TPU v7x, 32 devices: a whole 2x2x4 slice. The times are simulated.
32 devices in a mesh: ctx: 16 (over z, y, core), tp: 2 (over x).
Axes of the slice: x: 2, y: 2, z: 4, core: 2. Of those that a mesh axis runs over, the one named last changes fastest.
Arguments:
- query: bfloat16 [2048, 4096], P('ctx', 'tp'), may hold values from -6 to 6
- key_in: bfloat16 [2048, 4096], P('ctx', 'tp'), may hold values from -6 to 6
- value: bfloat16 [2048, 4096], P('ctx', 'tp'), may hold values from -6 to 6
- short_taps: float32 [3, 3, 4096], P(None, None, 'tp'), may hold values from -3.5 to 3.5
- skip_gain: float32 [4096], P('tp'), may hold values from -1 to 1
- filter_spectrum: float32 [2048, 2, 2, 4096], P('ctx', None, None, 'tp'), may hold values from -6 to 6
- out_weight: bfloat16 [4096, 4096], P('tp'), may hold values from -0.09375 to 0.09375
Outputs:
- mixed_out: bfloat16 [2048, 4096], P('ctx', 'tp')
All inputs are finite; a program needn't handle non-finite values.
Results may differ from a plain program's by a relative error of at most 0.0049.
Values may be sent and summed in bfloat16 or wider, within the bound.
No kernel may reach another device: no remote copies, remote signals or barrier semaphores. Data moves between devices by JAX's collectives and lax.ppermute only.
A program may use at most 128 MiB of HBM per device.

v0:
```python
import math

import jax
import jax.numpy as jnp
from jax import lax
from jax.experimental import pallas as pl
from jax.experimental.pallas import tpu as pltpu
from jax.sharding import PartitionSpec as P

RADIX = 8
ROWS = 16
LANES = 128


def shifted_in(rows, axis):
    count = lax.axis_size(axis)
    return lax.ppermute(rows, axis, [(i, i + 1) for i in range(count - 1)])


def causal_filter(signal, tail, taps):
    values = jnp.concatenate([tail, signal], axis=0).astype(jnp.float32)
    return taps[0] * values[2:] + taps[1] * values[1:-1] + taps[2] * values[:-2]


def turn(rows, columns, order):
    index = rows[:, None] * columns[None, :] % order
    angle = (2.0 * math.pi / order) * index.astype(jnp.float32)
    return jnp.cos(angle), jnp.sin(angle)


def exact_dot(left, right):
    return jnp.dot(left, right, precision=lax.Precision.HIGHEST, preferred_element_type=jnp.float32)


def radix_of(order):
    return 2 ** ((order.bit_length() - 1) // 2)


def long_filter(signal, spectrum_real, spectrum_imag):
    length, width = signal.shape
    order = spectrum_real.shape[0]
    radix = radix_of(order)
    span, depth = order // radix, length // radix
    low = jnp.arange(span, dtype=jnp.int32)
    deep = jnp.arange(depth, dtype=jnp.int32)
    lanes = jnp.arange(radix, dtype=jnp.int32)
    inner_cos, inner_sin = turn(low, deep, span)
    twiddle_cos, twiddle_sin = (t[:, :, None] for t in turn(lanes, low, order))
    outer_cos, outer_sin = turn(lanes, lanes, radix)

    samples = signal.astype(jnp.float32).reshape(depth, radix * width)
    real = exact_dot(inner_cos, samples).reshape(span, radix, width).transpose(1, 0, 2)
    imag = -exact_dot(inner_sin, samples).reshape(span, radix, width).transpose(1, 0, 2)
    real, imag = (
        (real * twiddle_cos + imag * twiddle_sin).reshape(radix, span * width),
        (imag * twiddle_cos - real * twiddle_sin).reshape(radix, span * width),
    )
    real, imag = (
        exact_dot(outer_cos, real) + exact_dot(outer_sin, imag),
        exact_dot(outer_cos, imag) - exact_dot(outer_sin, real),
    )
    spectrum_real = spectrum_real.astype(jnp.float32).reshape(radix, span * width)
    spectrum_imag = spectrum_imag.astype(jnp.float32).reshape(radix, span * width)
    real, imag = (
        real * spectrum_real - imag * spectrum_imag,
        real * spectrum_imag + imag * spectrum_real,
    )
    real, imag = (
        (exact_dot(outer_cos, real) - exact_dot(outer_sin, imag)).reshape(radix, span, width),
        (exact_dot(outer_cos, imag) + exact_dot(outer_sin, real)).reshape(radix, span, width),
    )
    real, imag = (
        (real * twiddle_cos - imag * twiddle_sin).transpose(1, 0, 2).reshape(span, radix * width),
        (imag * twiddle_cos + real * twiddle_sin).transpose(1, 0, 2).reshape(span, radix * width),
    )
    result = exact_dot(inner_cos.T, real) - exact_dot(inner_sin.T, imag)
    return (result / order).reshape(length, width)


def split(value):
    high = value.astype(jnp.bfloat16)
    return high, (value - high.astype(jnp.float32)).astype(jnp.bfloat16)


def butterfly(parts, sign):
    count = len(parts)
    if count == 1:
        return parts
    even, odd = butterfly(parts[0::2], sign), butterfly(parts[1::2], sign)
    half = count // 2
    low, high = [], []
    for j in range(half):
        real, imag = odd[j]
        if 4 * j == count:
            real, imag = (-imag, real) if sign > 0 else (imag, -real)
        elif j:
            c, s = math.cos(2.0 * math.pi * j / count), sign * math.sin(2.0 * math.pi * j / count)
            if 8 * j == count:
                real, imag = ((real - imag) * c, (real + imag) * c) if sign > 0 else ((real + imag) * c, (imag - real) * c)
            elif 8 * j == 3 * count:
                real, imag = ((real + imag) * c, (imag - real) * c) if sign > 0 else ((real - imag) * c, (real + imag) * c)
            else:
                real, imag = real * c - imag * s, real * s + imag * c
        low.append((even[j][0] + real, even[j][1] + imag))
        high.append((even[j][0] - real, even[j][1] - imag))
    return low + high


def transform_kernel(
    taken_ref, fwd_high, fwd_low, inv_high, inv_low, cos_ref, sin_ref, out_ref,
    samples, packed, inner, high_ref, low_ref,
):
    devices, tokens, block = out_ref.shape
    span = cos_ref.shape[1]
    depth = packed.shape[0]
    per_source = 2 * tokens

    for q in range(devices):
        samples[pl.ds(q * tokens, tokens), :] = taken_ref[q, pl.ds(0, tokens), :].astype(jnp.float32)
    for v in range(RADIX):
        packed[:, pl.ds(v * block, block)] = samples[pl.ds(v, depth, stride=RADIX), :].astype(jnp.bfloat16)

    wide = 2 * block

    @pl.loop(0, RADIX * block // wide)
    def _(i):
        lanes = pl.ds(pl.multiple_of(i * wide, wide), wide)
        right = packed[:, lanes]
        inner[:, lanes] = jnp.dot(fwd_high[...], right, preferred_element_type=jnp.float32) + jnp.dot(
            fwd_low[...], right, preferred_element_type=jnp.float32
        )

    @pl.loop(0, span // ROWS)
    def _(i):
        start = pl.multiple_of(i * ROWS, ROWS)
        rows, rows_imag = pl.ds(start, ROWS), pl.ds(pl.multiple_of(start + span, ROWS), ROWS)
        parts = []
        for v in range(RADIX):
            lanes = pl.ds(v * block, block)
            real, imag = inner[rows, lanes], inner[rows_imag, lanes]
            if v:
                c, s = cos_ref[v, rows, :], sin_ref[v, rows, :]
                real, imag = real * c - imag * s, -(imag * c + real * s)
            else:
                imag = -imag
            parts.append((real, imag))
        parts = butterfly(parts, -1)
        scaled = []
        for j in range(RADIX):
            place = start + j * span
            source, row = place // per_source, place % per_source
            real_rows = pl.ds(pl.multiple_of(tokens + row, ROWS), ROWS)
            imag_rows = pl.ds(pl.multiple_of(tokens + per_source + row, ROWS), ROWS)
            fr = taken_ref[source, real_rows, :].astype(jnp.float32)
            fi = taken_ref[source, imag_rows, :].astype(jnp.float32)
            real, imag = parts[j]
            scaled.append((real * fr - imag * fi, real * fi + imag * fr))
        parts = butterfly(scaled, 1)
        for v in range(RADIX):
            lanes = pl.ds(v * block, block)
            real, imag = parts[v]
            if v:
                c, s = cos_ref[v, rows, :], sin_ref[v, rows, :]
                real, imag = real * c - imag * s, imag * c + real * s
            high_ref[rows, lanes], low_ref[rows, lanes] = split(real)
            high_ref[rows_imag, lanes], low_ref[rows_imag, lanes] = split(-imag)

    for v in range(0, RADIX, 2):
        lanes = pl.ds(v * block, wide)
        right = high_ref[:, lanes]
        result = (
            jnp.dot(inv_high[...], right, preferred_element_type=jnp.float32)
            + jnp.dot(inv_low[...], right, preferred_element_type=jnp.float32)
            + jnp.dot(inv_high[...], low_ref[:, lanes], preferred_element_type=jnp.float32)
        ) * (0.5 / (devices * tokens))
        samples[pl.ds(v, depth, stride=RADIX), :] = result[:, :block]
        samples[pl.ds(v + 1, depth, stride=RADIX), :] = result[:, block:]
    for q in range(devices):
        out_ref[q, :, :] = samples[pl.ds(q * tokens, tokens), :].astype(jnp.bfloat16)


def local_tables(length, block):
    order = 2 * length
    span, depth = order // RADIX, length // RADIX
    low, deep, lanes = lax.optimization_barrier(
        tuple(jnp.arange(size, dtype=jnp.int32) for size in (span, depth, RADIX))
    )
    forward = jnp.concatenate(turn(low, deep, span), axis=0)
    inverse = jnp.concatenate(turn(deep, low, span), axis=1)
    twiddles = tuple(
        jnp.broadcast_to(t[:, :, None], (RADIX, span, block)) for t in turn(lanes, low, order)
    )
    return (*split(forward), *split(inverse), *twiddles)


def local_transform(taken, tables, tokens):
    devices, _, block = taken.shape
    length = devices * tokens
    span, depth = 2 * length // RADIX, length // RADIX
    flops = 5 * 2 * 2 * span * depth * RADIX * block
    return pl.pallas_call(
        transform_kernel,
        out_shape=jax.ShapeDtypeStruct((devices, tokens, block), jnp.bfloat16),
        in_specs=[pl.BlockSpec(memory_space=pltpu.VMEM)] * 7,
        out_specs=pl.BlockSpec(memory_space=pltpu.VMEM),
        scratch_shapes=[
            pltpu.VMEM((length, block), jnp.float32),
            pltpu.VMEM((depth, RADIX * block), jnp.bfloat16),
            pltpu.VMEM((2 * span, RADIX * block), jnp.float32),
            pltpu.VMEM((2 * span, RADIX * block), jnp.bfloat16),
            pltpu.VMEM((2 * span, RADIX * block), jnp.bfloat16),
        ],
        compiler_params=pltpu.CompilerParams(vmem_limit_bytes=40 * 2**20),
        cost_estimate=pl.CostEstimate(flops=flops, bytes_accessed=taken.size * 2, transcendentals=0),
    )(taken, *tables)


def sum_shares(share, axis):
    count = lax.axis_size(axis)
    rank = lax.axis_index(axis)
    columns = share.shape[1] // count
    total = lax.dynamic_slice_in_dim(share, rank * columns, columns, axis=1)
    for step in range(1, count):
        piece = lax.dynamic_slice_in_dim(share, (rank + step) % count * columns, columns, axis=1)
        pairs = [(i, (i + step) % count) for i in range(count)]
        total = total + lax.ppermute(piece.astype(jnp.bfloat16), axis, pairs).astype(jnp.float32)
    return total


def shards(query, key_in, value, short_taps, skip_gain, filter_spectrum, out_weight):
    devices = lax.axis_size("ctx")
    tokens, channels = query.shape
    length, block = tokens * devices, channels // devices
    tails = shifted_in(jnp.concatenate([query[-2:], key_in[-2:], value[-2:]], axis=0), "ctx")
    gate_signal = causal_filter(query, tails[0:2], short_taps[0])
    mixed_in = causal_filter(key_in, tails[2:4], short_taps[1]) * causal_filter(
        value, tails[4:6], short_taps[2]
    )
    own_signal = mixed_in.astype(jnp.bfloat16).reshape(tokens, devices, block).transpose(1, 0, 2)
    own_spectrum = (
        filter_spectrum.astype(jnp.bfloat16)
        .reshape(tokens, 2, 2, devices, block)
        .transpose(3, 2, 0, 1, 4)
        .reshape(devices, 4 * tokens, block)
    )
    sent = jnp.concatenate([own_signal, own_spectrum], axis=1)
    taken = lax.all_to_all(sent, "ctx", split_axis=0, concat_axis=0, tiled=True)
    if block == LANES:
        convolved = local_transform(taken, local_tables(length, block), tokens)
    else:
        signal = taken[:, :tokens].reshape(length, block)
        spectrum_real = taken[:, tokens : 3 * tokens].reshape(2 * length, block)
        spectrum_imag = taken[:, 3 * tokens :].reshape(2 * length, block)
        convolved = long_filter(signal, spectrum_real, spectrum_imag).astype(jnp.bfloat16)
    convolved = lax.all_to_all(
        convolved.reshape(devices, tokens, block), "ctx", split_axis=0, concat_axis=0, tiled=True
    )
    convolved = convolved.transpose(1, 0, 2).reshape(tokens, channels).astype(jnp.float32)
    gated = (gate_signal * (convolved + skip_gain * mixed_in)).astype(jnp.bfloat16)
    share = jnp.dot(gated, out_weight, preferred_element_type=jnp.float32)
    return sum_shares(share, "tp").astype(jnp.bfloat16)


def solution(mesh):
    return jax.shard_map(
        shards,
        mesh=mesh,
        in_specs=(
            P("ctx", "tp"),
            P("ctx", "tp"),
            P("ctx", "tp"),
            P(None, None, "tp"),
            P("tp"),
            P("ctx", None, None, "tp"),
            P("tp", None),
        ),
        out_specs=P("ctx", "tp"),
        check_vma=False,
    )
```

profile of v0, /device:TPU:0, one launch (start us, length us, event | category | flops | bytes accessed | tf_op | source)
XLA Modules:
  0.0 154.1 jit_solution(2718262519723560884)
XLA Ops:
  2.4 1.1 copy.18
  3.5 2.4 %collective-permute-start = (bf16[6,2048]{0,1:T(8,128)(2,1)}, bf16[6,2048]{0,1:T(8,128)(2,1)S(1)}, u32[]{:S(2)}, u32[]{:S(2)}) collective-permute-start(bf16[6,2048]{0,1:T(8,128)(2,1)} %copy.18), channel_id=1, source_target_pairs={{0,2},{2,4},{4,6},{6,8},{8,10},{10,12},{12,14},{14,16},{16,18},{18... | collective-permute-start | bytes 73736 | tf_op jit(solution)/shard_map/ppermute | solution.py:17
  6.9 1.3 copy.20
  8.2 1.0 copy.21
  9.2 4.3 %convert_element_type.74 = bf16[128,2,2,2048]{3,2,1,0:T(2,128)(2,1)S(1)} convert(f32[128,2,2,2048]{3,2,1,0:T(2,128)} %param.12) | non-fusion elementwise | flops 1048576 | bytes 6291456 | tf_op jit(solution)/shard_map/convert_element_type | solution.py:241
  13.5 2.6 %reshape.98 = bf16[128,2,2,16,128]{4,3,2,1,0:T(8,128)(2,1)} reshape(bf16[128,2,2,2048]{3,2,1,0:T(2,128)(2,1)S(1)} %convert_element_type.74) | data formatting | bytes 4194304 | tf_op jit(solution)/shard_map/reshape | solution.py:242
  16.2 3.8 %copy.23 = bf16[128,2,2,16,128]{4,1,0,2,3:T(2,128)(2,1)S(1)} copy(bf16[128,2,2,16,128]{4,3,2,1,0:T(8,128)(2,1)} %reshape.98) | data formatting | bytes 4194304 | tf_op jit(solution)/shard_map/reshape | solution.py:242
  20.0 1.1 fusion.28
  21.9 3.8 %fusion.26 = (bf16[128,2048]{0,1:T(8,128)(2,1)S(1)}, f32[128,2048]{0,1:T(8,128)}) fusion(f32[130,2048]{0,1:T(8,128)S(1)} %get-tuple-element.32, f32[2048]{0:T(1024)S(1)} %bitcast.32, f32[2048]{0:T(1024)S(1)} %bitcast.33, f32[2048]{0:T(1024)S(1)} %bitcast.28, f32[130,2048]{0,1:T(8,128)S(1)} %get-tuple-element.31, f32[2048]{0:T(1024)S(1)} %bitcast.29, ...), kind=kLoop, calls=%fused_computation.63 | loop fusion | flops 3145728 | bytes 7913472 | tf_op jit(solution)/shard_map/convert_element_type | solution.py:239
  25.9 1.7 %pad_maximum_fusion = bf16[16,640,128]{2,1,0:T(8,128)(2,1)} fusion(bf16[16,512,128]{2,1,0:T(8,128)(2,1)S(1)} %bitcast.22, bf16[16,128,128]{2,1,0:T(8,128)(2,1)S(1)} %bitcast.23), kind=kLoop, calls=%fused_computation | loop fusion | flops 5242880 | bytes 5242880 | tf_op jit(solution)/shard_map/concatenate | solution.py:246
  27.6 7.2 %all-to-all-start = ((bf16[16,640,128]{2,1,0:T(8,128)(2,1)}), bf16[16,640,128]{2,1,0:T(8,128)(2,1)S(1)}, u32[]{:S(2)}, u32[]{:S(2)}) async-start(bf16[16,640,128]{2,1,0:T(8,128)(2,1)} %pad_maximum_fusion), calls=%async_computation | async-start | bytes 5242880 | tf_op jit(solution)/shard_map/all_to_all | solution.py:247
  34.8 2.1 %fusion.18 = (f32[256,512]{1,0:T(8,128)S(1)}, f32[256,512]{1,0:T(8,128)S(1)}) fusion(s32[512]{0:T(512)S(1)} %iota.9, s32[256]{0:T(256)S(1)} %iota.10), kind=kLoop, calls=%fused_computation.49 | loop fusion | flops 1835008 | bytes 1051648 | tf_op jit(solution)/shard_map/cos | solution.py:28
  37.9 2.1 %fusion.20 = (f32[512,256]{1,0:T(8,128)S(1)}, f32[512,256]{1,0:T(8,128)S(1)}) fusion(s32[256]{0:T(256)S(1)} %iota.10, s32[512]{0:T(512)S(1)} %iota.9), kind=kLoop, calls=%fused_computation.51 | loop fusion | flops 1835008 | bytes 1051648 | tf_op jit(solution)/shard_map/cos | solution.py:28
  41.9 43.0 %all-to-all-done.taken_ref = bf16[16,640,128]{2,1,0:T(8,128)(2,1)S(1)} async-done(((bf16[16,640,128]{2,1,0:T(8,128)(2,1)}), bf16[16,640,128]{2,1,0:T(8,128)(2,1)S(1)}, u32[]{:S(2)}, u32[]{:S(2)}) %all-to-all-start) | async-done | bytes 2621472 | tf_op jit(solution)/shard_map/all_to_all | solution.py:247
  86.3 8.1 %shard_map.73 = bf16[16,128,128]{2,1,0:T(8,128)(2,1)S(1)} custom-call(bf16[16,640,128]{2,1,0:T(8,128)(2,1)S(1)} %all-to-all-done.taken_ref, bf16[1024,256]{1,0:T(8,128)(2,1)S(1)} %copy-done.1, bf16[1024,256]{1,0:T(8,128)(2,1)S(1)} %copy-done.2, bf16[256,1024]{1,0:T(8,128)(2,1)S(1)} %fusion.9.inv_high, bf16[256,1024]{1,0:T(8,128)(2,1)S(1)} %copy-done, ...), custom_call_target="tpu_custom_call" | custom-call | flops 2684354560 | bytes 2621440 | tf_op jit(solution)/shard_map/pallas_call | solution.py:201
  95.1 13.5 %all-to-all-start.1 = ((bf16[16,128,128]{2,1,0:T(8,128)(2,1)}), bf16[16,128,128]{2,1,0:T(8,128)(2,1)}, u32[]{:S(2)}, u32[]{:S(2)}) async-start(bf16[16,128,128]{2,1,0:T(8,128)(2,1)} %copy-done.3), calls=%async_computation.1 | async-start | bytes 1048576 | tf_op jit(solution)/shard_map/all_to_all | solution.py:255
  108.7 1.3 copy.19
  110.5 12.5 %all-to-all-done.1 = bf16[16,128,128]{2,1,0:T(8,128)(2,1)} async-done(((bf16[16,128,128]{2,1,0:T(8,128)(2,1)}), bf16[16,128,128]{2,1,0:T(8,128)(2,1)}, u32[]{:S(2)}, u32[]{:S(2)}) %all-to-all-start.1) | async-done | bytes 524320 | tf_op jit(solution)/shard_map/all_to_all | solution.py:255
  123.0 2.1 %convert_bitcast_fusion = f32[128,16,128]{2,0,1:T(8,128)} fusion(bf16[16,128,128]{2,1,0:T(8,128)(2,1)} %all-to-all-done.1), kind=kLoop, calls=%fused_computation.25 | loop fusion | flops 262144 | bytes 1572864 | tf_op jit(solution)/shard_map/convert_element_type | solution.py:258
  125.1 2.5 %copy.24 = f32[128,16,128]{0,2,1:T(8,128)} copy(f32[128,16,128]{2,0,1:T(8,128)} %convert_bitcast_fusion) | data formatting | bytes 2097152 | tf_op jit(solution)/shard_map/convert_element_type | solution.py:258
  127.6 3.2 %fusion.7 = bf16[128,2048]{0,1:T(8,128)(2,1)S(1)} fusion(f32[130,2048]{0,1:T(8,128)S(1)} %maximum_convert_fusion, f32[128,16,128]{0,2,1:T(8,128)} %copy.24, f32[128,2048]{0,1:T(8,128)S(1)} %copy-done.4, f32[2048]{0:T(1024)S(1)} %copy-done.8, f32[2048]{0:T(1024)S(1)} %bitcast.26, f32[2048]{0:T(1024)S(1)} %bitcast.27, f32[2048]{0:T(1024)S(1)} %bitcast.25), kind=kLoop, calls=%fused_computation.15 | loop fusion | flops 2359296 | bytes 5799936 | tf_op jit(solution)/shard_map/convert_element_type | solution.py:259
  130.9 8.2 %fusion.30 = f32[128,4096]{1,0:T(8,128)S(1)} fusion(bf16[128,2048]{0,1:T(8,128)(2,1)S(1)} %fusion.7, bf16[2048,4096]{1,0:T(8,128)(2,1)} %param.13), kind=kOutput, calls=%fused_computation.66 | convolution fusion | flops 2147483648 | bytes 19398656 | tf_op jit(solution)/shard_map/dot_general | solution.py:260
  139.1 1.6 %collective-permute-start.1 = (bf16[128,2048]{1,0:T(8,128)(2,1)S(1)}, bf16[128,2048]{1,0:T(8,128)(2,1)S(1)}, u32[]{:S(2)}, u32[]{:S(2)}) collective-permute-start(bf16[128,2048]{1,0:T(8,128)(2,1)S(1)} %dynamic-slice_convert_fusion), channel_id=1, source_target_pairs={{0,1},{1,0},{2,3},{3,2},{4,5},{5,4},{6,7},{7,6},{8,9},{9,8},{10,11... | collective-permute-start | bytes 1572872 | tf_op jit(solution)/shard_map/ppermute | solution.py:226
  140.7 12.5 %collective-permute-done.1 = bf16[128,2048]{1,0:T(8,128)(2,1)S(1)} collective-permute-done((bf16[128,2048]{1,0:T(8,128)(2,1)S(1)}, bf16[128,2048]{1,0:T(8,128)(2,1)S(1)}, u32[]{:S(2)}, u32[]{:S(2)}) %collective-permute-start.1) | collective-permute-done | bytes 524320 | tf_op jit(solution)/shard_map/ppermute | solution.py:226
  (39 shorter events, 10.8 us)
Async XLA Ops:
  0.0 8.2 %copy-start.7 = (bf16[128,2048]{1,0:T(8,128)(2,1)S(1)}, bf16[128,2048]{1,0:T(8,128)(2,1)}, u32[]{:S(2)}) copy-start(bf16[128,2048]{1,0:T(8,128)(2,1)} %param.9) | copy-start | bytes 1572868
  3.5 16.5 %collective-permute-start = (bf16[6,2048]{0,1:T(8,128)(2,1)}, bf16[6,2048]{0,1:T(8,128)(2,1)S(1)}, u32[]{:S(2)}, u32[]{:S(2)}) collective-permute-start(bf16[6,2048]{0,1:T(8,128)(2,1)} %copy.18), channel_id=1, source_target_pairs={{0,2},{2,4},{4,6},{6,8},{8,10},{10,12},{12,14},{14,16},{16,18},{18... | collective-permute-start | bytes 73736 | tf_op jit(solution)/shard_map/ppermute | solution.py:17
  20.0 1.1 copy-start.5
  27.6 57.3 %all-to-all-start = ((bf16[16,640,128]{2,1,0:T(8,128)(2,1)}), bf16[16,640,128]{2,1,0:T(8,128)(2,1)S(1)}, u32[]{:S(2)}, u32[]{:S(2)}) async-start(bf16[16,640,128]{2,1,0:T(8,128)(2,1)} %pad_maximum_fusion), calls=%async_computation | async-start | bytes 5242880 | tf_op jit(solution)/shard_map/all_to_all | solution.py:247
  84.9 1.2 copy-start
  84.9 1.2 copy-start.1
  84.9 1.4 copy-start.2
  94.3 0.8 copy-start.3
  95.1 14.9 %copy-start.6 = (bf16[2,2048]{0,1:T(8,128)(2,1)S(1)}, bf16[2,2048]{0,1:T(8,128)(2,1)}, u32[]{:S(2)}) copy-start(bf16[2,2048]{0,1:T(8,128)(2,1)} %get-tuple-element.15) | copy-start | bytes 24580
  95.1 27.8 %all-to-all-start.1 = ((bf16[16,128,128]{2,1,0:T(8,128)(2,1)}), bf16[16,128,128]{2,1,0:T(8,128)(2,1)}, u32[]{:S(2)}, u32[]{:S(2)}) async-start(bf16[16,128,128]{2,1,0:T(8,128)(2,1)} %copy-done.3), calls=%async_computation.1 | async-start | bytes 1048576 | tf_op jit(solution)/shard_map/all_to_all | solution.py:255
  110.4 17.2 %copy-start.4 = (f32[128,2048]{0,1:T(8,128)S(1)}, f32[128,2048]{0,1:T(8,128)}, u32[]{:S(2)}) copy-start(f32[128,2048]{0,1:T(8,128)} %get-tuple-element.12) | copy-start | bytes 3145732
  110.4 17.2 %copy-start.8 = (f32[2048]{0:T(1024)S(1)}, f32[2048]{0:T(1024)}, u32[]{:S(2)}) copy-start(f32[2048]{0:T(1024)} %param.11) | copy-start | bytes 24580
  139.1 14.0 %collective-permute-start.1 = (bf16[128,2048]{1,0:T(8,128)(2,1)S(1)}, bf16[128,2048]{1,0:T(8,128)(2,1)S(1)}, u32[]{:S(2)}, u32[]{:S(2)}) collective-permute-start(bf16[128,2048]{1,0:T(8,128)(2,1)S(1)} %dynamic-slice_convert_fusion), channel_id=1, source_target_pairs={{0,1},{1,0},{2,3},{3,2},{4,5},{5,4},{6,7},{7,6},{8,9},{9,8},{10,11... | collective-permute-start | bytes 1572872 | tf_op jit(solution)/shard_map/ppermute | solution.py:226
where the time goes:
time: 155 us; the launch traced here: 154 us
  waiting for transfers between devices  68 us (44%)
  starting transfers between devices  24.7 us (16%)
  other arithmetic  24.3 us (16%)
  local copies, waits for them, and re-layouts  20.6 us (13%)
  matrix products  8.16 us (5%)
  Pallas kernels  8.05 us (5%)
    all_to_all x1, waiting for transfers between devices, shards(): taken = lax.all_to_all(sent, 'ctx', split_axis=0, concat_axis=0, tiled=True)  43 us
    all_to_all x1, starting transfers between devices, shards(): lax.all_to_all(convolved.reshape(devices, tokens, block), 'ctx', split_ax...  13.5 us
    all_to_all x1, waiting for transfers between devices, shards(): lax.all_to_all(convolved.reshape(devices, tokens, block), 'ctx', split_ax...  12.5 us
    ppermute x1, waiting for transfers between devices, sum_shares(): lax.ppermute(piece.astype(jnp.bfloat16), axis, pairs).astype(jnp.float32)  12.5 us
    dot_general x1, matrix products, shards(): share = jnp.dot(gated, out_weight, preferred_element_type=jnp.float32)  8.16 us
    pallas_call x1, Pallas kernels, local_transform(): pl.pallas_call(transform_kernel, out_shape=jax.ShapeDtypeStruct((devices,...  8.05 us
    all_to_all x1, starting transfers between devices, shards(): taken = lax.all_to_all(sent, 'ctx', split_axis=0, concat_axis=0, tiled=True)  7.18 us
    reshape x2, local copies, waits for them, and re-layouts, shards(): own_spectrum = filter_spectrum.astype(jnp.bfloat16).reshape(tokens, 2, 2,...  6.45 us
  transfers between devices with their start and end apart: 4, of which 3 were waited for; matrix products, arithmetic and copies ran while one was open for 15% of the time, Pallas kernels for 0%

commit v1 on v0

--- a/solution.py
+++ b/solution.py
@@ -10,6 +10,7 @@
 RADIX = 8
 ROWS = 16
 LANES = 128
+WIDTH = 512
 
 
 def shifted_in(rows, axis):
@@ -80,6 +81,180 @@
 def split(value):
     high = value.astype(jnp.bfloat16)
     return high, (value - high.astype(jnp.float32)).astype(jnp.bfloat16)
+
+
+def split_table(value):
+    high = lax.reduce_precision(value, exponent_bits=8, mantissa_bits=7)
+    return high.astype(jnp.bfloat16), (value - high).astype(jnp.bfloat16)
+
+
+def filtered_block(signal_ref, tails_ref, taps_ref, which, lanes):
+    values = signal_ref[:, lanes].astype(jnp.float32)
+    tails = tails_ref[:, lanes].astype(jnp.float32)
+    older, newer = tails[2 * which : 2 * which + 1], tails[2 * which + 1 : 2 * which + 2]
+    row = lax.broadcasted_iota(jnp.int32, values.shape, 0)
+    one_back = jnp.where(row == 0, newer, pltpu.roll(values, 1, 0))
+    two_back = jnp.where(row == 0, older, jnp.where(row == 1, newer, pltpu.roll(values, 2, 0)))
+    taps = taps_ref[which, :, lanes]
+    return taps[0:1] * values + taps[1:2] * one_back + taps[2:3] * two_back
+
+
+def pack_kernel(spectrum_ref, sent_ref, staged):
+    pairs, group, _ = spectrum_ref.shape
+    tokens = sent_ref.shape[1] - 2 * pairs
+    staged[...] = spectrum_ref[...].reshape(staged.shape)
+    for d in range(group // 2):
+        for r in range(2):
+            sent_ref[d, pl.ds(tokens + r * pairs, pairs), :] = staged[
+                pl.ds(2 * d + r, pairs, stride=group), :
+            ].astype(jnp.bfloat16)
+
+
+def packed_spectrum(filter_spectrum, devices):
+    tokens, _, _, channels = filter_spectrum.shape
+    block = channels // devices
+    pairs = 2 * tokens
+    view = (
+        filter_spectrum.reshape(tokens, 2, 2, devices, block)
+        .transpose(0, 1, 3, 2, 4)
+        .reshape(pairs, 2 * devices, block)
+    )
+    rows = tokens + 2 * pairs
+    return pl.pallas_call(
+        pack_kernel,
+        grid=(devices // 4,),
+        out_shape=jax.ShapeDtypeStruct((devices, rows, block), jnp.bfloat16),
+        in_specs=[pl.BlockSpec((pairs, 8, block), lambda i: (0, i, 0))],
+        out_specs=pl.BlockSpec((4, rows, block), lambda i: (i, 0, 0)),
+        scratch_shapes=[pltpu.VMEM((pairs * 8, block), jnp.float32)],
+        compiler_params=pltpu.CompilerParams(vmem_limit_bytes=16 * 2**20),
+        cost_estimate=pl.CostEstimate(
+            flops=0, bytes_accessed=view.size * 6, transcendentals=0
+        ),
+    )(view)
+
+
+def mix_kernel(key_ref, value_ref, tails_ref, taps_ref, _, sent_ref):
+    devices, _, block = sent_ref.shape
+    for j in range(devices):
+        lanes = pl.ds(j * block, block)
+        mixed = filtered_block(key_ref, tails_ref, taps_ref, 1, lanes) * filtered_block(
+            value_ref, tails_ref, taps_ref, 2, lanes
+        )
+        sent_ref[j] = mixed.astype(jnp.bfloat16)
+
+
+def with_signal(key_in, value, tails, short_taps, sent):
+    devices, _, block = sent.shape
+    tokens = key_in.shape[0]
+    whole = pl.BlockSpec(memory_space=pltpu.VMEM)
+    return pl.pallas_call(
+        mix_kernel,
+        grid=(1,),
+        out_shape=jax.ShapeDtypeStruct(sent.shape, sent.dtype),
+        in_specs=[whole] * 4 + [pl.BlockSpec(memory_space=pl.ANY)],
+        out_specs=pl.BlockSpec((devices, tokens, block), lambda i: (0, 0, 0)),
+        input_output_aliases={4: 0},
+        compiler_params=pltpu.CompilerParams(vmem_limit_bytes=16 * 2**20),
+        cost_estimate=pl.CostEstimate(
+            flops=12 * key_in.size, bytes_accessed=6 * key_in.size, transcendentals=0
+        ),
+    )(key_in, value, tails, short_taps, sent)
+
+
+def gate_kernel(query_ref, key_ref, value_ref, tails_ref, taps_ref, gain_ref, gate_ref, direct_ref):
+    tokens, channels = query_ref.shape
+    for j in range(channels // LANES):
+        lanes = pl.ds(j * LANES, LANES)
+        mixed = filtered_block(key_ref, tails_ref, taps_ref, 1, lanes) * filtered_block(
+            value_ref, tails_ref, taps_ref, 2, lanes
+        )
+        gate_ref[:, lanes] = filtered_block(query_ref, tails_ref, taps_ref, 0, lanes)
+        direct_ref[:, lanes] = gain_ref[:, lanes] * mixed
+
+
+def gates(query, key_in, value, tails, short_taps, skip_gain):
+    shape = jax.ShapeDtypeStruct(query.shape, jnp.float32)
+    whole = pl.BlockSpec(memory_space=pltpu.VMEM)
+    return pl.pallas_call(
+        gate_kernel,
+        out_shape=(shape, shape),
+        in_specs=[whole] * 6,
+        out_specs=(whole, whole),
+        compiler_params=pltpu.CompilerParams(vmem_limit_bytes=16 * 2**20),
+        cost_estimate=pl.CostEstimate(
+            flops=20 * query.size, bytes_accessed=14 * query.size, transcendentals=0
+        ),
+    )(query, key_in, value, tails, short_taps, skip_gain[None, :])
+
+
+def columns_of(rank, count, columns, width):
+    return pl.ds(pl.multiple_of(rank * columns + count * width, width), width)
+
+
+def far_kernel(conv_ref, gate_ref, direct_ref, weight_ref, gated_ref, share_ref):
+    devices, _, block = conv_ref.shape
+    columns = share_ref.shape[1]
+    for j in range(devices):
+        lanes = pl.ds(j * block, block)
+        gated_ref[:, lanes] = (
+            gate_ref[:, lanes] * (conv_ref[j].astype(jnp.float32) + direct_ref[:, lanes])
+        ).astype(jnp.bfloat16)
+    other = 1 - lax.axis_index("tp")
+
+    @pl.loop(0, columns // WIDTH)
+    def _(i):
+        place = pl.ds(pl.multiple_of(i * WIDTH, WIDTH), WIDTH)
+        share_ref[:, place] = jnp.dot(
+            gated_ref[...],
+            weight_ref[:, columns_of(other, i, columns, WIDTH)],
+            preferred_element_type=jnp.float32,
+        ).astype(jnp.bfloat16)
+
+
+def near_kernel(gated_ref, weight_ref, share_ref):
+    columns = share_ref.shape[1]
+    rank = lax.axis_index("tp")
+
+    @pl.loop(0, columns // WIDTH)
+    def _(i):
+        place = pl.ds(pl.multiple_of(i * WIDTH, WIDTH), WIDTH)
+        share_ref[:, place] = jnp.dot(
+            gated_ref[...],
+            weight_ref[:, columns_of(rank, i, columns, WIDTH)],
+            preferred_element_type=jnp.float32,
+        )
+
+
+def projected(convolved, gate_signal, direct, out_weight):
+    tokens, channels = gate_signal.shape
+    columns = out_weight.shape[1] // 2
+    whole = pl.BlockSpec(memory_space=pltpu.VMEM)
+    cost = pl.CostEstimate(
+        flops=2 * tokens * channels * columns, bytes_accessed=2 * channels * columns, transcendentals=0
+    )
+    params = pltpu.CompilerParams(vmem_limit_bytes=40 * 2**20)
+    gated, far = pl.pallas_call(
+        far_kernel,
+        out_shape=(
+            jax.ShapeDtypeStruct((tokens, channels), jnp.bfloat16),
+            jax.ShapeDtypeStruct((tokens, columns), jnp.bfloat16),
+        ),
+        in_specs=[whole] * 4,
+        out_specs=(whole, whole),
+        compiler_params=params,
+        cost_estimate=cost,
+    )(convolved, gate_signal, direct, out_weight)
+    arrived = lax.ppermute(far, "tp", [(0, 1), (1, 0)])
+    near = pl.pallas_call(
+        near_kernel,
+        out_shape=jax.ShapeDtypeStruct((tokens, columns), jnp.float32),
+        in_specs=[whole] * 2,
+        out_specs=whole,
+        compiler_params=params,
+        cost_estimate=cost,
+    )(gated, out_weight)
+    return (near + arrived.astype(jnp.float32)).astype(jnp.bfloat16)
 
 
 def butterfly(parts, sign):
@@ -190,7 +365,7 @@
     twiddles = tuple(
         jnp.broadcast_to(t[:, :, None], (RADIX, span, block)) for t in turn(lanes, low, order)
     )
-    return (*split(forward), *split(inverse), *twiddles)
+    return (*split_table(forward), *split_table(inverse), *twiddles)
 
 
 def local_transform(taken, tables, tokens):
@@ -227,10 +402,26 @@
     return total
 
 
+def fused_shards(query, key_in, value, short_taps, skip_gain, filter_spectrum, out_weight):
+    devices = lax.axis_size("ctx")
+    tokens, channels = query.shape
+    tails = shifted_in(jnp.concatenate([query[-2:], key_in[-2:], value[-2:]], axis=0), "ctx")
+    sent = packed_spectrum(filter_spectrum, devices)
+    sent = with_signal(key_in, value, tails, short_taps, sent)
+    taken = lax.all_to_all(sent, "ctx", split_axis=0, concat_axis=0, tiled=True)
+    gate_signal, direct = gates(query, key_in, value, tails, short_taps, skip_gain)
+    tables = local_tables(tokens * devices, channels // devices)
+    convolved = local_transform(taken, tables, tokens)
+    convolved = lax.all_to_all(convolved, "ctx", split_axis=0, concat_axis=0, tiled=True)
+    return projected(convolved, gate_signal, direct, out_weight)
+
+
 def shards(query, key_in, value, short_taps, skip_gain, filter_spectrum, out_weight):
     devices = lax.axis_size("ctx")
     tokens, channels = query.shape
     length, block = tokens * devices, channels // devices
+    if block == LANES and devices % 4 == 0 and lax.axis_size("tp") == 2:
+        return fused_shards(query, key_in, value, short_taps, skip_gain, filter_spectrum, out_weight)
     tails = shifted_in(jnp.concatenate([query[-2:], key_in[-2:], value[-2:]], axis=0), "ctx")
     gate_signal = causal_filter(query, tails[0:2], short_taps[0])
     mixed_in = causal_filter(key_in, tails[2:4], short_taps[1]) * causal_filter(
@@ -245,13 +436,10 @@
     )
     sent = jnp.concatenate([own_signal, own_spectrum], axis=1)
     taken = lax.all_to_all(sent, "ctx", split_axis=0, concat_axis=0, tiled=True)
-    if block == LANES:
-        convolved = local_transform(taken, local_tables(length, block), tokens)
-    else:
-        signal = taken[:, :tokens].reshape(length, block)
-        spectrum_real = taken[:, tokens : 3 * tokens].reshape(2 * length, block)
-        spectrum_imag = taken[:, 3 * tokens :].reshape(2 * length, block)
-        convolved = long_filter(signal, spectrum_real, spectrum_imag).astype(jnp.bfloat16)
+    signal = taken[:, :tokens].reshape(length, block)
+    spectrum_real = taken[:, tokens : 3 * tokens].reshape(2 * length, block)
+    spectrum_imag = taken[:, 3 * tokens :].reshape(2 * length, block)
+    convolved = long_filter(signal, spectrum_real, spectrum_imag).astype(jnp.bfloat16)
     convolved = lax.all_to_all(
         convolved.reshape(devices, tokens, block), "ctx", split_axis=0, concat_axis=0, tiled=True
     )

time: 155 us -> 130 us (0.84)
  Pallas kernels: 8.05 us -> 29 us
  other arithmetic: 24.3 us -> 7.62 us
  local copies, waits for them, and re-layouts: 20.6 us -> 8.87 us
  waiting for transfers between devices: 68 us -> 59.3 us
  matrix products: 8.16 us -> 0 us
    pallas_call x0 -> x5, Pallas kernels: none -> 21 us  [the longest x1 7.77 us: projected(): pl.pallas_call(far_kernel, out_shape=(jax.ShapeDtypeStruct((tokens, chann...]
    convert_element_type x11 -> x3, other arithmetic: 18.2 us -> 3.2 us  [the longest x2 2.3 us: split_table(): return (high.astype(jnp.bfloat16), (value - high).astype(jnp.bfloat16))]
    dot_general x1 -> x0, matrix products: 8.16 us -> none  [shards(): share = jnp.dot(gated, out_weight, preferred_element_type=jnp.float32)]
    ppermute x1, waiting for transfers between devices: 12.5 us -> 4.88 us  [projected(): arrived = lax.ppermute(far, 'tp', [(0, 1), (1, 0)])]
    reshape x3 -> x0, local copies, waits for them, and re-layouts: 6.73 us -> none  [the longest x2 6.45 us: shards(): own_spectrum = filter_spectrum.astype(jnp.bfloat16).reshape(tokens, 2, 2,...]
    convert_element_type x2 -> x0, local copies, waits for them, and re-layouts: 2.6 us -> none  [the longest x1 2.54 us: shards(): convolved.transpose(1, 0, 2).reshape(tokens, channels).astype(jnp.float32)]
    slice x5 -> x3, local copies, waits for them, and re-layouts: 4.47 us -> 2.31 us  [the longest x1 0.77 us: fused_shards(): key_in[-2:]]
    concatenate x2 -> x1, other arithmetic: 1.71 us -> 0.03 us  [fused_shards(): jnp.concatenate([query[-2:], key_in[-2:], value[-2:]], axis=0)]
  transfers between devices with their start and end apart: 4 -> 4, of which waited for: 3 -> 3; matrix products, arithmetic and copies ran while one was open for 15% -> 5% of each run, Pallas kernels for 0% -> 9%
where the time goes in v1:
time: 130 us
  waiting for transfers between devices  59.3 us (46%)
  Pallas kernels  29 us (22%)
  starting transfers between devices  24.5 us (19%)
  local copies, waits for them, and re-layouts  8.87 us (7%)
  other arithmetic  7.62 us (6%)
    all_to_all x1, waiting for transfers between devices, fused_shards(): taken = lax.all_to_all(sent, 'ctx', split_axis=0, concat_axis=0, tiled=True)  43.4 us
    all_to_all x1, starting transfers between devices, fused_shards(): lax.all_to_all(convolved, 'ctx', split_axis=0, concat_axis=0, tiled=True)  13.3 us
    all_to_all x1, waiting for transfers between devices, fused_shards(): lax.all_to_all(convolved, 'ctx', split_axis=0, concat_axis=0, tiled=True)  11.1 us
    pallas_call x1, Pallas kernels, local_transform(): pl.pallas_call(transform_kernel, out_shape=jax.ShapeDtypeStruct((devices,...  8.05 us
    pallas_call x1, Pallas kernels, projected(): pl.pallas_call(far_kernel, out_shape=(jax.ShapeDtypeStruct((tokens, chann...  7.77 us
    pallas_call x1, Pallas kernels, projected(): pl.pallas_call(near_kernel, out_shape=jax.ShapeDtypeStruct((tokens, colum...  7.61 us
    all_to_all x1, starting transfers between devices, fused_shards(): taken = lax.all_to_all(sent, 'ctx', split_axis=0, concat_axis=0, tiled=True)  7.21 us
    unnamed x24, local copies, waits for them, and re-layouts  5.35 us
  transfers between devices with their start and end apart: 4, of which 3 were waited for; matrix products, arithmetic and copies ran while one was open for 5% of the time, Pallas kernels for 9%

profile of v1, /device:TPU:0, one launch (start us, length us, event | category | flops | bytes accessed | tf_op | source)
XLA Modules:
  0.0 129.5 jit_solution(5757202164952297470)
XLA Ops:
  0.8 0.8 slice.10
  1.5 0.8 slice.9
  2.4 2.4 %collective-permute-start = (bf16[6,2048]{1,0:T(8,128)(2,1)S(1)}, bf16[6,2048]{1,0:T(8,128)(2,1)S(1)}, u32[]{:S(2)}, u32[]{:S(2)}) collective-permute-start(bf16[6,2048]{1,0:T(8,128)(2,1)S(1)} %pad_maximum_fusion.2), channel_id=1, source_target_pairs={{0,2},{2,4},{4,6},{6,8},{8,10},{10,12},{12,14},{14,16},{16,18},{18... | collective-permute-start | bytes 73736 | tf_op jit(solution)/shard_map/ppermute | solution.py:18
  4.8 2.2 %copy-done = f32[128,2,2,2048]{3,2,1,0:T(2,128)S(1)} copy-done((f32[128,2,2,2048]{3,2,1,0:T(2,128)S(1)}, f32[128,2,2,2048]{3,2,1,0:T(2,128)}, u32[]{:S(2)}) %copy-start) | copy-done | bytes 4194328
  7.0 2.9 %shard_map.73._ = bf16[16,640,128]{2,1,0:T(8,128)(2,1)} custom-call(f32[256,32,128]{2,1,0:T(8,128)S(1)} %bitcast.6), custom_call_target="tpu_custom_call" | custom-call | bytes 6291456 | tf_op jit(solution)/shard_map/pallas_call | solution.py:123
  9.9 1.6 %shard_map.74 = bf16[16,640,128]{2,1,0:T(8,128)(2,1)} custom-call(bf16[128,2048]{1,0:T(8,128)(2,1)S(1)} %copy-done.1, bf16[128,2048]{1,0:T(8,128)(2,1)S(1)} %copy-done.2, bf16[6,2048]{1,0:T(8,128)(2,1)S(1)} %collective-permute-done.tails_ref, f32[3,3,2048]{2,1,0:T(4,128)S(1)} %copy-done.10, ...), custom_call_target="tpu_custom_call", output_to_operand_aliasing={{}: (4, {})} | custom-call | flops 3145728 | bytes 1572864 | tf_op jit(solution)/shard_map/pallas_call | solution.py:151
  11.5 7.2 %all-to-all-start = ((bf16[16,640,128]{2,1,0:T(8,128)(2,1)}), bf16[16,640,128]{2,1,0:T(8,128)(2,1)S(1)}, u32[]{:S(2)}, u32[]{:S(2)}) async-start(bf16[16,640,128]{2,1,0:T(8,128)(2,1)} %shard_map.74), calls=%async_computation | async-start | bytes 5242880 | tf_op jit(solution)/shard_map/all_to_all | solution.py:411
  18.7 2.1 %fusion.11 = (f32[512,256]{1,0:T(8,128)S(1)}, f32[512,256]{1,0:T(8,128)S(1)}) fusion(s32[256]{0:T(256)S(1)} %iota.10, s32[512]{0:T(512)S(1)} %iota.9), kind=kLoop, calls=%fused_computation.28 | loop fusion | flops 1835008 | bytes 1051648 | tf_op jit(solution)/shard_map/cos | solution.py:29
  20.8 1.1 fusion
  22.0 2.1 %fusion.9 = (f32[256,512]{1,0:T(8,128)S(1)}, f32[256,512]{1,0:T(8,128)S(1)}) fusion(s32[512]{0:T(512)S(1)} %iota.9, s32[256]{0:T(256)S(1)} %iota.10), kind=kLoop, calls=%fused_computation.26 | loop fusion | flops 1835008 | bytes 1051648 | tf_op jit(solution)/shard_map/cos | solution.py:29
  24.1 1.2 fusion.1
  25.4 43.4 %all-to-all-done.taken_ref = bf16[16,640,128]{2,1,0:T(8,128)(2,1)S(1)} async-done(((bf16[16,640,128]{2,1,0:T(8,128)(2,1)}), bf16[16,640,128]{2,1,0:T(8,128)(2,1)S(1)}, u32[]{:S(2)}, u32[]{:S(2)}) %all-to-all-start) | async-done | bytes 2621472 | tf_op jit(solution)/shard_map/all_to_all | solution.py:411
  70.3 8.1 %shard_map.75 = bf16[16,128,128]{2,1,0:T(8,128)(2,1)S(1)} custom-call(bf16[16,640,128]{2,1,0:T(8,128)(2,1)S(1)} %all-to-all-done.taken_ref, bf16[1024,256]{1,0:T(8,128)(2,1)S(1)} %copy-done.7, bf16[1024,256]{1,0:T(8,128)(2,1)S(1)} %copy-done.6, bf16[256,1024]{1,0:T(8,128)(2,1)S(1)} %copy-done.9, bf16[256,1024]{1,0:T(8,128)(2,1)S(1)} %copy-done.8, ...), custom_call_target="tpu_custom_call" | custom-call | flops 2684354560 | bytes 2621440 | tf_op jit(solution)/shard_map/pallas_call | solution.py:376
  78.4 0.8 copy-done.5
  79.2 13.3 %all-to-all-start.1 = ((bf16[16,128,128]{2,1,0:T(8,128)(2,1)}), bf16[16,128,128]{2,1,0:T(8,128)(2,1)S(1)}, u32[]{:S(2)}, u32[]{:S(2)}) async-start(bf16[16,128,128]{2,1,0:T(8,128)(2,1)} %copy-done.5), calls=%async_computation.1 | async-start | bytes 1048576 | tf_op jit(solution)/shard_map/all_to_all | solution.py:415
  92.5 1.0 copy-done.3
  93.6 1.0 copy-done.4
  94.6 1.1 shard_map.76
  95.7 11.1 %all-to-all-done.1.conv_ref = bf16[16,128,128]{2,1,0:T(8,128)(2,1)S(1)} async-done(((bf16[16,128,128]{2,1,0:T(8,128)(2,1)}), bf16[16,128,128]{2,1,0:T(8,128)(2,1)S(1)}, u32[]{:S(2)}, u32[]{:S(2)}) %all-to-all-start.1) | async-done | bytes 524320 | tf_op jit(solution)/shard_map/all_to_all | solution.py:415
  106.8 7.8 %shard_map.77 = (bf16[128,2048]{1,0:T(8,128)(2,1)S(1)}, bf16[128,2048]{1,0:T(8,128)(2,1)S(1)}) custom-call(bf16[16,128,128]{2,1,0:T(8,128)(2,1)S(1)} %all-to-all-done.1.conv_ref, f32[128,2048]{1,0:T(8,128)S(1)} %get-tuple-element.15.gate_ref, f32[128,2048]{1,0:T(8,128)S(1)} %get-tuple-element.16.direct_ref, bf16[2048,4096]{1,0:T(8,128)(2,1)} %weight_ref.3), custom_call_target="tpu_custom_call" | custom-call | flops 1073741824 | bytes 8388608 | tf_op jit(solution)/shard_map/pallas_call | solution.py:237
  114.6 1.6 %collective-permute-start.1 = (bf16[128,2048]{1,0:T(8,128)(2,1)S(1)}, bf16[128,2048]{1,0:T(8,128)(2,1)S(1)}, u32[]{:S(2)}, u32[]{:S(2)}) collective-permute-start(bf16[128,2048]{1,0:T(8,128)(2,1)S(1)} %get-tuple-element.18), channel_id=1, source_target_pairs={{0,1},{1,0},{2,3},{3,2},{4,5},{5,4},{6,7},{7,6},{8,9},{9,8},{10,11... | collective-permute-start | bytes 1572872 | tf_op jit(solution)/shard_map/ppermute | solution.py:248
  116.1 7.6 %shard_map.78 = f32[128,2048]{1,0:T(8,128)S(1)} custom-call(bf16[128,2048]{1,0:T(8,128)(2,1)S(1)} %get-tuple-element.17.gated_ref, bf16[2048,4096]{1,0:T(8,128)(2,1)} %weight_ref.3), custom_call_target="tpu_custom_call" | custom-call | flops 1073741824 | bytes 8388608 | tf_op jit(solution)/shard_map/pallas_call | solution.py:249
  123.7 4.9 %collective-permute-done.1 = bf16[128,2048]{1,0:T(8,128)(2,1)S(1)} collective-permute-done((bf16[128,2048]{1,0:T(8,128)(2,1)S(1)}, bf16[128,2048]{1,0:T(8,128)(2,1)S(1)}, u32[]{:S(2)}, u32[]{:S(2)}) %collective-permute-start.1) | collective-permute-done | bytes 524320 | tf_op jit(solution)/shard_map/ppermute | solution.py:248
  128.6 0.9 add_convert_fusion
  (29 shorter events, 2.5 us)
Async XLA Ops:
  2.4 7.5 %collective-permute-start = (bf16[6,2048]{1,0:T(8,128)(2,1)S(1)}, bf16[6,2048]{1,0:T(8,128)(2,1)S(1)}, u32[]{:S(2)}, u32[]{:S(2)}) collective-permute-start(bf16[6,2048]{1,0:T(8,128)(2,1)S(1)} %pad_maximum_fusion.2), channel_id=1, source_target_pairs={{0,2},{2,4},{4,6},{6,8},{8,10},{10,12},{12,14},{14,16},{16,18},{18... | collective-permute-start | bytes 73736 | tf_op jit(solution)/shard_map/ppermute | solution.py:18
  4.8 2.2 %copy-start = (f32[128,2,2,2048]{3,2,1,0:T(2,128)S(1)}, f32[128,2,2,2048]{3,2,1,0:T(2,128)}, u32[]{:S(2)}) copy-start(f32[128,2,2,2048]{3,2,1,0:T(2,128)} %param.12) | copy-start | bytes 12582916
  7.0 2.9 %copy-start.1 = (bf16[128,2048]{1,0:T(8,128)(2,1)S(1)}, bf16[128,2048]{1,0:T(8,128)(2,1)}, u32[]{:S(2)}) copy-start(bf16[128,2048]{1,0:T(8,128)(2,1)} %key_ref.3) | copy-start | bytes 1572868
  7.0 2.9 %copy-start.2 = (bf16[128,2048]{1,0:T(8,128)(2,1)S(1)}, bf16[128,2048]{1,0:T(8,128)(2,1)}, u32[]{:S(2)}) copy-start(bf16[128,2048]{1,0:T(8,128)(2,1)} %value_ref.3) | copy-start | bytes 1572868
  7.0 2.9 %copy-start.10 = (f32[3,3,2048]{2,1,0:T(4,128)S(1)}, f32[3,3,2048]{2,1,0:T(4,128)}, u32[]{:S(2)}) copy-start(f32[3,3,2048]{2,1,0:T(4,128)} %taps_ref.3) | copy-start | bytes 221188
  11.5 57.3 %all-to-all-start = ((bf16[16,640,128]{2,1,0:T(8,128)(2,1)}), bf16[16,640,128]{2,1,0:T(8,128)(2,1)S(1)}, u32[]{:S(2)}, u32[]{:S(2)}) async-start(bf16[16,640,128]{2,1,0:T(8,128)(2,1)} %shard_map.74), calls=%async_computation | async-start | bytes 5242880 | tf_op jit(solution)/shard_map/all_to_all | solution.py:411
  68.8 1.2 copy-start.6
  68.8 1.2 copy-start.7
  68.8 1.4 %copy-start.8 = (bf16[256,1024]{1,0:T(8,128)(2,1)S(1)}, bf16[256,1024]{1,0:T(8,128)(2,1)}, u32[]{:S(2)}) copy-start(bf16[256,1024]{1,0:T(8,128)(2,1)} %get-tuple-element.19.inv_low) | copy-start | bytes 1572868
  68.8 1.5 %copy-start.9 = (bf16[256,1024]{1,0:T(8,128)(2,1)S(1)}, bf16[256,1024]{1,0:T(8,128)(2,1)}, u32[]{:S(2)}) copy-start(bf16[256,1024]{1,0:T(8,128)(2,1)} %get-tuple-element.20.inv_high) | copy-start | bytes 1572868
  70.3 22.2 %copy-start.11 = (f32[2048]{0:T(1024)S(1)}, f32[2048]{0:T(1024)}, u32[]{:S(2)}) copy-start(f32[2048]{0:T(1024)} %param.11) | copy-start | bytes 24580
  78.4 0.8 copy-start.5
  79.2 27.6 %all-to-all-start.1 = ((bf16[16,128,128]{2,1,0:T(8,128)(2,1)}), bf16[16,128,128]{2,1,0:T(8,128)(2,1)S(1)}, u32[]{:S(2)}, u32[]{:S(2)}) async-start(bf16[16,128,128]{2,1,0:T(8,128)(2,1)} %copy-done.5), calls=%async_computation.1 | async-start | bytes 1048576 | tf_op jit(solution)/shard_map/all_to_all | solution.py:415
  92.5 1.0 copy-start.3
  93.6 1.0 copy-start.4
  114.6 14.1 %collective-permute-start.1 = (bf16[128,2048]{1,0:T(8,128)(2,1)S(1)}, bf16[128,2048]{1,0:T(8,128)(2,1)S(1)}, u32[]{:S(2)}, u32[]{:S(2)}) collective-permute-start(bf16[128,2048]{1,0:T(8,128)(2,1)S(1)} %get-tuple-element.18), channel_id=1, source_target_pairs={{0,1},{1,0},{2,3},{3,2},{4,5},{5,4},{6,7},{7,6},{8,9},{9,8},{10,11... | collective-permute-start | bytes 1572872 | tf_op jit(solution)/shard_map/ppermute | solution.py:248

commit v2 on v1

--- a/solution.py
+++ b/solution.py
@@ -99,6 +99,25 @@
     return taps[0:1] * values + taps[1:2] * one_back + taps[2:3] * two_back
 
 
+def tails_kernel(query_ref, key_ref, value_ref, tails_ref):
+    rows = query_ref.shape[0]
+    for which, ref in enumerate((query_ref, key_ref, value_ref)):
+        tails_ref[2 * which : 2 * which + 2, :] = ref[...].astype(jnp.float32)[rows - 2 :].astype(jnp.bfloat16)
+
+
+def own_tails(query, key_in, value):
+    tokens, channels = query.shape
+    last = pl.BlockSpec((ROWS, channels), lambda i: (tokens // ROWS - 1, 0))
+    return pl.pallas_call(
+        tails_kernel,
+        grid=(1,),
+        out_shape=jax.ShapeDtypeStruct((6, channels), query.dtype),
+        in_specs=[last] * 3,
+        out_specs=pl.BlockSpec((6, channels), lambda i: (0, 0)),
+        compiler_params=pltpu.CompilerParams(vmem_limit_bytes=4 * 2**20),
+    )(*(pltpu.with_memory_space_constraint(a, pltpu.HBM) for a in (query, key_in, value)))
+
+
 def pack_kernel(spectrum_ref, sent_ref, staged):
     pairs, group, _ = spectrum_ref.shape
     tokens = sent_ref.shape[1] - 2 * pairs
@@ -120,6 +139,7 @@
         .reshape(pairs, 2 * devices, block)
     )
     rows = tokens + 2 * pairs
+    view = pltpu.with_memory_space_constraint(view, pltpu.HBM)
     return pl.pallas_call(
         pack_kernel,
         grid=(devices // 4,),
@@ -188,41 +208,43 @@
     )(query, key_in, value, tails, short_taps, skip_gain[None, :])
 
 
-def columns_of(rank, count, columns, width):
-    return pl.ds(pl.multiple_of(rank * columns + count * width, width), width)
-
-
-def far_kernel(conv_ref, gate_ref, direct_ref, weight_ref, gated_ref, share_ref):
+def chunk_copies(weight_ref, held, sems, rank):
+    chunks, _, width = held.shape
+    return [
+        pltpu.make_async_copy(
+            weight_ref.at[:, pl.ds(pl.multiple_of((rank * chunks + i) * width, width), width)],
+            held.at[i],
+            sems.at[i],
+        )
+        for i in range(chunks)
+    ]
+
+
+def far_kernel(conv_ref, gate_ref, direct_ref, weight_ref, gated_ref, share_ref, held, sems):
     devices, _, block = conv_ref.shape
-    columns = share_ref.shape[1]
+    copies = chunk_copies(weight_ref, held, sems, 1 - lax.axis_index("tp"))
+    for copy in copies:
+        copy.start()
     for j in range(devices):
         lanes = pl.ds(j * block, block)
         gated_ref[:, lanes] = (
             gate_ref[:, lanes] * (conv_ref[j].astype(jnp.float32) + direct_ref[:, lanes])
         ).astype(jnp.bfloat16)
-    other = 1 - lax.axis_index("tp")
-
-    @pl.loop(0, columns // WIDTH)
-    def _(i):
-        place = pl.ds(pl.multiple_of(i * WIDTH, WIDTH), WIDTH)
-        share_ref[:, place] = jnp.dot(
-            gated_ref[...],
-            weight_ref[:, columns_of(other, i, columns, WIDTH)],
-            preferred_element_type=jnp.float32,
+    for i, copy in enumerate(copies):
+        copy.wait()
+        share_ref[:, pl.ds(i * WIDTH, WIDTH)] = jnp.dot(
+            gated_ref[...], held[i], preferred_element_type=jnp.float32
         ).astype(jnp.bfloat16)
 
 
-def near_kernel(gated_ref, weight_ref, share_ref):
-    columns = share_ref.shape[1]
-    rank = lax.axis_index("tp")
-
-    @pl.loop(0, columns // WIDTH)
-    def _(i):
-        place = pl.ds(pl.multiple_of(i * WIDTH, WIDTH), WIDTH)
-        share_ref[:, place] = jnp.dot(
-            gated_ref[...],
-            weight_ref[:, columns_of(rank, i, columns, WIDTH)],
-            preferred_element_type=jnp.float32,
+def near_kernel(gated_ref, weight_ref, share_ref, held, sems):
+    copies = chunk_copies(weight_ref, held, sems, lax.axis_index("tp"))
+    for copy in copies:
+        copy.start()
+    for i, copy in enumerate(copies):
+        copy.wait()
+        share_ref[:, pl.ds(i * WIDTH, WIDTH)] = jnp.dot(
+            gated_ref[...], held[i], preferred_element_type=jnp.float32
         )
 
 
@@ -233,26 +255,33 @@
     cost = pl.CostEstimate(
         flops=2 * tokens * channels * columns, bytes_accessed=2 * channels * columns, transcendentals=0
     )
-    params = pltpu.CompilerParams(vmem_limit_bytes=40 * 2**20)
+    common = {
+        "scratch_shapes": [
+            pltpu.VMEM((columns // WIDTH, channels, WIDTH), jnp.bfloat16),
+            pltpu.SemaphoreType.DMA((columns // WIDTH,)),
+        ],
+        "compiler_params": pltpu.CompilerParams(vmem_limit_bytes=20 * 2**20),
+        "cost_estimate": cost,
+    }
+    out_weight = pltpu.with_memory_space_constraint(out_weight, pltpu.HBM)
+    remote = pl.BlockSpec(memory_space=pltpu.HBM)
     gated, far = pl.pallas_call(
         far_kernel,
         out_shape=(
             jax.ShapeDtypeStruct((tokens, channels), jnp.bfloat16),
             jax.ShapeDtypeStruct((tokens, columns), jnp.bfloat16),
         ),
-        in_specs=[whole] * 4,
+        in_specs=[whole] * 3 + [remote],
         out_specs=(whole, whole),
-        compiler_params=params,
-        cost_estimate=cost,
+        **common,
     )(convolved, gate_signal, direct, out_weight)
     arrived = lax.ppermute(far, "tp", [(0, 1), (1, 0)])
     near = pl.pallas_call(
         near_kernel,
         out_shape=jax.ShapeDtypeStruct((tokens, columns), jnp.float32),
-        in_specs=[whole] * 2,
+        in_specs=[whole, remote],
         out_specs=whole,
-        compiler_params=params,
-        cost_estimate=cost,
+        **common,
     )(gated, out_weight)
     return (near + arrived.astype(jnp.float32)).astype(jnp.bfloat16)
 
@@ -281,64 +310,111 @@
     return low + high
 
 
+def turned(pair, cosine, sine):
+    real, imag = pair
+    return real * cosine - imag * sine, imag * cosine + real * sine
+
+
+def scaled(pair, factor):
+    return turned(pair, *factor)
+
+
 def transform_kernel(
-    taken_ref, fwd_high, fwd_low, inv_high, inv_low, cos_ref, sin_ref, out_ref,
-    samples, packed, inner, high_ref, low_ref,
+    taken_ref, *refs,
 ):
-    devices, tokens, block = out_ref.shape
-    span = cos_ref.shape[1]
+    tables, out_ref = refs[:6], refs[6]
+    samples, packed, inner, flipped, high_ref, low_ref, done, sem = refs[7:15]
+    held, table_sems = refs[15:21], refs[21]
+    fwd_high, fwd_low, inv_high, inv_low, cos_ref, sin_ref = held
+    loads = [pltpu.make_async_copy(*p, table_sems.at[i]) for i, p in enumerate(zip(tables, held))]
+    for load in loads:
+        load.start()
+    devices, tokens, block = done.shape
     depth = packed.shape[0]
-    per_source = 2 * tokens
+    half = cos_ref.shape[1]
+    lane = [pl.ds(v * block, block) for v in range(RADIX)]
+    spectrum_real, spectrum_imag = pl.ds(tokens, half), pl.ds(tokens + half, half)
 
     for q in range(devices):
         samples[pl.ds(q * tokens, tokens), :] = taken_ref[q, pl.ds(0, tokens), :].astype(jnp.float32)
     for v in range(RADIX):
-        packed[:, pl.ds(v * block, block)] = samples[pl.ds(v, depth, stride=RADIX), :].astype(jnp.bfloat16)
+        packed[:, lane[v]] = samples[pl.ds(v, depth, stride=RADIX), :].astype(jnp.bfloat16)
 
     wide = 2 * block
-
-    @pl.loop(0, RADIX * block // wide)
-    def _(i):
-        lanes = pl.ds(pl.multiple_of(i * wide, wide), wide)
+    loads[0].wait()
+    loads[1].wait()
+    for v in range(0, RADIX, 2):
+        lanes = pl.ds(v * block, wide)
         right = packed[:, lanes]
         inner[:, lanes] = jnp.dot(fwd_high[...], right, preferred_element_type=jnp.float32) + jnp.dot(
             fwd_low[...], right, preferred_element_type=jnp.float32
         )
 
-    @pl.loop(0, span // ROWS)
-    def _(i):
-        start = pl.multiple_of(i * ROWS, ROWS)
-        rows, rows_imag = pl.ds(start, ROWS), pl.ds(pl.multiple_of(start + span, ROWS), ROWS)
-        parts = []
+    row = lax.broadcasted_iota(jnp.int32, (half, half), 0)
+    column = lax.broadcasted_iota(jnp.int32, (half, half), 1)
+    flip = jnp.where(row + column == half, 1.0, 0.0).astype(jnp.bfloat16)
+    for j in range(RADIX):
+        source = 2 * RADIX - 1 - 2 * j
+        right = jnp.concatenate(
+            [taken_ref[source, spectrum_real, :], taken_ref[source, spectrum_imag, :]], axis=1
+        )
+        flipped[j] = jnp.dot(flip, right, preferred_element_type=jnp.float32).astype(jnp.bfloat16)
+
+    def products(rows, start, parts):
+        parts = butterfly(parts, -1)
+        result = []
+        for j in range(RADIX):
+            real = taken_ref[2 * j, pl.ds(start + tokens, ROWS), :].astype(jnp.float32)
+            imag = taken_ref[2 * j, pl.ds(start + tokens + half, ROWS), :].astype(jnp.float32)
+            mirror = flipped[j, rows, :].astype(jnp.float32)
+            result.append(scaled(parts[j], (real + mirror[:, :block], imag - mirror[:, block:])))
+        return butterfly(result, 1)
+
+    def middle(start, first):
+        rows = pl.ds(start, ROWS)
+        rows_imag = pl.ds(start + half, ROWS)
+        top = lax.broadcasted_iota(jnp.int32, (ROWS, block), 0) == 0
+        parts, tops = [], []
         for v in range(RADIX):
-            lanes = pl.ds(v * block, block)
-            real, imag = inner[rows, lanes], inner[rows_imag, lanes]
+            real, imag = inner[rows, lane[v]], -inner[rows_imag, lane[v]]
+            if first:
+                tops.append(-imag)
+                imag = jnp.where(top, 0.0, imag)
             if v:
-                c, s = cos_ref[v, rows, :], sin_ref[v, rows, :]
-                real, imag = real * c - imag * s, -(imag * c + real * s)
-            else:
-                imag = -imag
+                real, imag = turned((real, imag), cos_ref[v, rows, :], -sin_ref[v, rows, :])
             parts.append((real, imag))
-        parts = butterfly(parts, -1)
-        scaled = []
-        for j in range(RADIX):
-            place = start + j * span
-            source, row = place // per_source, place % per_source
-            real_rows = pl.ds(pl.multiple_of(tokens + row, ROWS), ROWS)
-            imag_rows = pl.ds(pl.multiple_of(tokens + per_source + row, ROWS), ROWS)
-            fr = taken_ref[source, real_rows, :].astype(jnp.float32)
-            fi = taken_ref[source, imag_rows, :].astype(jnp.float32)
-            real, imag = parts[j]
-            scaled.append((real * fr - imag * fi, real * fi + imag * fr))
-        parts = butterfly(scaled, 1)
+        parts = products(rows, start, parts)
+        if first:
+            angles = [math.pi * v / RADIX for v in range(RADIX)]
+            nyquist = [(t * math.cos(a), t * -math.sin(a)) for t, a in zip(tops, angles)]
+            nyquist = butterfly(nyquist, -1)
+            nyquist = [
+                scaled(
+                    nyquist[j],
+                    (
+                        taken_ref[2 * j + 1, pl.ds(tokens, ROWS), :].astype(jnp.float32),
+                        taken_ref[2 * j + 1, pl.ds(tokens + half, ROWS), :].astype(jnp.float32),
+                    ),
+                )
+                for j in range(RADIX)
+            ]
+            nyquist = butterfly(nyquist, 1)
+            tops = [n[0] * math.cos(a) - n[1] * math.sin(a) for n, a in zip(nyquist, angles)]
         for v in range(RADIX):
-            lanes = pl.ds(v * block, block)
             real, imag = parts[v]
             if v:
-                c, s = cos_ref[v, rows, :], sin_ref[v, rows, :]
-                real, imag = real * c - imag * s, imag * c + real * s
-            high_ref[rows, lanes], low_ref[rows, lanes] = split(real)
-            high_ref[rows_imag, lanes], low_ref[rows_imag, lanes] = split(-imag)
+                real, imag = turned((real, imag), cos_ref[v, rows, :], sin_ref[v, rows, :])
+            imag = jnp.where(top, tops[v], -imag) if first else -imag
+            high_ref[rows, lane[v]], low_ref[rows, lane[v]] = split(real)
+            high_ref[rows_imag, lane[v]], low_ref[rows_imag, lane[v]] = split(imag)
+
+    for load in loads[2:]:
+        load.wait()
+    middle(0, True)
+
+    @pl.loop(1, half // ROWS)
+    def _(i):
+        middle(pl.multiple_of(i * ROWS, ROWS), False)
 
     for v in range(0, RADIX, 2):
         lanes = pl.ds(v * block, wide)
@@ -351,41 +427,89 @@
         samples[pl.ds(v, depth, stride=RADIX), :] = result[:, :block]
         samples[pl.ds(v + 1, depth, stride=RADIX), :] = result[:, block:]
     for q in range(devices):
-        out_ref[q, :, :] = samples[pl.ds(q * tokens, tokens), :].astype(jnp.bfloat16)
+        done[q] = samples[pl.ds(q * tokens, tokens), :].astype(jnp.bfloat16)
+    copy = pltpu.make_async_copy(done, out_ref, sem)
+    copy.start()
+    copy.wait()
+
+
+def angles_of(shape, rows, columns, order):
+    index = lax.broadcasted_iota(jnp.int32, shape, rows) * lax.broadcasted_iota(jnp.int32, shape, columns)
+    return (2.0 * math.pi / order) * (index & (order - 1)).astype(jnp.float32)
+
+
+def tables_kernel(fwd_high, fwd_low, inv_high, inv_low, cos_ref, sin_ref):
+    depth = fwd_high.shape[1]
+    _, half, block = cos_ref.shape
+    order = 2 * RADIX * half
+
+    def alternating(shape, dim):
+        return (1 - 2 * (lax.broadcasted_iota(jnp.int32, shape, dim) & 1)).astype(jnp.float32)
+
+    def first(shape, dim):
+        return lax.broadcasted_iota(jnp.int32, shape, dim) == 0
+
+    shape = (half, depth)
+    angle = angles_of(shape, 0, 1, 2 * half)
+    fwd_high[:half], fwd_low[:half] = split(jnp.cos(angle))
+    sine = jnp.where(first(shape, 0), alternating(shape, 1), jnp.sin(angle))
+    fwd_high[half:], fwd_low[half:] = split(sine)
+    shape = (depth, half)
+    angle = angles_of(shape, 0, 1, 2 * half)
+    inv_high[:, :half], inv_low[:, :half] = split(jnp.cos(angle))
+    sine = jnp.where(first(shape, 1), alternating(shape, 0), jnp.sin(angle))
+    inv_high[:, half:], inv_low[:, half:] = split(sine)
+
+    for v in range(RADIX):
+        step = lax.broadcasted_iota(jnp.int32, (half, block), 0).astype(jnp.float32)
+        angle = (2.0 * math.pi * v / order) * step
+        cos_ref[v] = jnp.cos(angle)
+        sin_ref[v] = jnp.sin(angle)
 
 
 def local_tables(length, block):
-    order = 2 * length
-    span, depth = order // RADIX, length // RADIX
-    low, deep, lanes = lax.optimization_barrier(
-        tuple(jnp.arange(size, dtype=jnp.int32) for size in (span, depth, RADIX))
-    )
-    forward = jnp.concatenate(turn(low, deep, span), axis=0)
-    inverse = jnp.concatenate(turn(deep, low, span), axis=1)
-    twiddles = tuple(
-        jnp.broadcast_to(t[:, :, None], (RADIX, span, block)) for t in turn(lanes, low, order)
-    )
-    return (*split_table(forward), *split_table(inverse), *twiddles)
+    half, depth = length // RADIX, length // RADIX
+    whole = pl.BlockSpec(memory_space=pltpu.VMEM)
+    forward = jax.ShapeDtypeStruct((2 * half, depth), jnp.bfloat16)
+    inverse = jax.ShapeDtypeStruct((depth, 2 * half), jnp.bfloat16)
+    twiddle = jax.ShapeDtypeStruct((RADIX, half, block), jnp.float32)
+    return pl.pallas_call(
+        tables_kernel,
+        out_shape=(forward, forward, inverse, inverse, twiddle, twiddle),
+        out_specs=(whole,) * 6,
+        compiler_params=pltpu.CompilerParams(vmem_limit_bytes=16 * 2**20),
+        cost_estimate=pl.CostEstimate(
+            flops=200 * RADIX * half * block, bytes_accessed=8 * RADIX * half * block, transcendentals=0
+        ),
+    )()
 
 
 def local_transform(taken, tables, tokens):
     devices, _, block = taken.shape
     length = devices * tokens
-    span, depth = 2 * length // RADIX, length // RADIX
-    flops = 5 * 2 * 2 * span * depth * RADIX * block
+    half, depth = length // RADIX, length // RADIX
+    flops = 5 * 2 * 2 * half * depth * RADIX * block
+    whole, remote = pl.BlockSpec(memory_space=pltpu.VMEM), pl.BlockSpec(memory_space=pltpu.HBM)
+    wide = RADIX * block
+    tables = [pltpu.with_memory_space_constraint(t, pltpu.HBM) for t in tables]
     return pl.pallas_call(
         transform_kernel,
-        out_shape=jax.ShapeDtypeStruct((devices, tokens, block), jnp.bfloat16),
-        in_specs=[pl.BlockSpec(memory_space=pltpu.VMEM)] * 7,
-        out_specs=pl.BlockSpec(memory_space=pltpu.VMEM),
+        out_shape=pltpu.HBM((devices, tokens, block), jnp.bfloat16),
+        in_specs=[whole] + [remote] * 6,
+        out_specs=remote,
         scratch_shapes=[
             pltpu.VMEM((length, block), jnp.float32),
-            pltpu.VMEM((depth, RADIX * block), jnp.bfloat16),
-            pltpu.VMEM((2 * span, RADIX * block), jnp.float32),
-            pltpu.VMEM((2 * span, RADIX * block), jnp.bfloat16),
-            pltpu.VMEM((2 * span, RADIX * block), jnp.bfloat16),
+            pltpu.VMEM((depth, wide), jnp.bfloat16),
+            pltpu.VMEM((2 * half, wide), jnp.float32),
+            pltpu.VMEM((RADIX, half, 2 * block), jnp.bfloat16),
+            pltpu.VMEM((2 * half, wide), jnp.bfloat16),
+            pltpu.VMEM((2 * half, wide), jnp.bfloat16),
+            pltpu.VMEM((devices, tokens, block), jnp.bfloat16),
+            pltpu.SemaphoreType.DMA,
+            *(pltpu.VMEM(t.shape, t.dtype) for t in tables),
+            pltpu.SemaphoreType.DMA((len(tables),)),
         ],
-        compiler_params=pltpu.CompilerParams(vmem_limit_bytes=40 * 2**20),
+        compiler_params=pltpu.CompilerParams(vmem_limit_bytes=20 * 2**20),
         cost_estimate=pl.CostEstimate(flops=flops, bytes_accessed=taken.size * 2, transcendentals=0),
     )(taken, *tables)
 
@@ -405,7 +529,7 @@
 def fused_shards(query, key_in, value, short_taps, skip_gain, filter_spectrum, out_weight):
     devices = lax.axis_size("ctx")
     tokens, channels = query.shape
-    tails = shifted_in(jnp.concatenate([query[-2:], key_in[-2:], value[-2:]], axis=0), "ctx")
+    tails = shifted_in(own_tails(query, key_in, value), "ctx")
     sent = packed_spectrum(filter_spectrum, devices)
     sent = with_signal(key_in, value, tails, short_taps, sent)
     taken = lax.all_to_all(sent, "ctx", split_axis=0, concat_axis=0, tiled=True)
@@ -420,7 +544,7 @@
     devices = lax.axis_size("ctx")
     tokens, channels = query.shape
     length, block = tokens * devices, channels // devices
-    if block == LANES and devices % 4 == 0 and lax.axis_size("tp") == 2:
+    if block == LANES and devices == 2 * RADIX and lax.axis_size("tp") == 2:
         return fused_shards(query, key_in, value, short_taps, skip_gain, filter_spectrum, out_weight)
     tails = shifted_in(jnp.concatenate([query[-2:], key_in[-2:], value[-2:]], axis=0), "ctx")
     gate_signal = causal_filter(query, tails[0:2], short_taps[0])

time: 130 us -> 120 us (0.923)
  other arithmetic: 7.62 us -> 0.9 us
  local copies, waits for them, and re-layouts: 8.87 us -> 6.86 us
  Pallas kernels: 29 us -> 27.3 us
    cos x2 -> x0, other arithmetic: 4.23 us -> none  [turn(): return (jnp.cos(angle), jnp.sin(angle))]
    pallas_call x1, Pallas kernels: 7.77 us -> 4.02 us  [projected(): pl.pallas_call(far_kernel, out_shape=(jax.ShapeDtypeStruct((tokens, chann...]
    pallas_call x1 -> x3, Pallas kernels: 8.05 us -> 11.8 us  [the longest x1 5.87 us: local_transform(): pl.pallas_call(transform_kernel, out_shape=pltpu.HBM((devices, tokens, bl...]
    pallas_call x1, Pallas kernels: 7.61 us -> 4 us  [projected(): pl.pallas_call(near_kernel, out_shape=jax.ShapeDtypeStruct((tokens, colum...]
    ppermute x1, waiting for transfers between devices: 4.88 us -> 8.48 us  [projected(): arrived = lax.ppermute(far, 'tp', [(0, 1), (1, 0)])]
    all_to_all x1, waiting for transfers between devices: 43.4 us -> 40.3 us  [fused_shards(): taken = lax.all_to_all(sent, 'ctx', split_axis=0, concat_axis=0, tiled=True)]
    slice x3 -> x0, local copies, waits for them, and re-layouts: 2.31 us -> none  [the longest x1 0.77 us: fused_shards(): key_in[-2:]]
    convert_element_type x2 -> x0, other arithmetic: 2.3 us -> none  [split_table(): return (high.astype(jnp.bfloat16), (value - high).astype(jnp.bfloat16))]
  transfers between devices with their start and end apart: 4 -> 4, of which waited for: 3 -> 3; matrix products, arithmetic and copies ran while one was open for 5% -> 0% of each run, Pallas kernels for 9% -> 12%
where the time goes in v2:
time: 120 us
  waiting for transfers between devices  59.9 us (50%)
  Pallas kernels  27.3 us (23%)
  starting transfers between devices  24.5 us (20%)
  local copies, waits for them, and re-layouts  6.86 us (6%)
    all_to_all x1, waiting for transfers between devices, fused_shards(): taken = lax.all_to_all(sent, 'ctx', split_axis=0, concat_axis=0, tiled=True)  40.3 us
    all_to_all x1, starting transfers between devices, fused_shards(): lax.all_to_all(convolved, 'ctx', split_axis=0, concat_axis=0, tiled=True)  13.3 us
    all_to_all x1, waiting for transfers between devices, fused_shards(): lax.all_to_all(convolved, 'ctx', split_axis=0, concat_axis=0, tiled=True)  11 us
    ppermute x1, waiting for transfers between devices, projected(): arrived = lax.ppermute(far, 'tp', [(0, 1), (1, 0)])  8.48 us
    all_to_all x1, starting transfers between devices, fused_shards(): taken = lax.all_to_all(sent, 'ctx', split_axis=0, concat_axis=0, tiled=True)  7.21 us
    unnamed x24, local copies, waits for them, and re-layouts  6.86 us
    pallas_call x1, Pallas kernels, local_transform(): pl.pallas_call(transform_kernel, out_shape=pltpu.HBM((devices, tokens, bl...  5.87 us
    pallas_call x1, Pallas kernels, local_tables(): pl.pallas_call(tables_kernel, out_shape=(forward, forward, inverse, inver...  4.99 us
  transfers between devices with their start and end apart: 4, of which 3 were waited for; matrix products, arithmetic and copies ran while one was open for 0% of the time, Pallas kernels for 12%

profile of v2, /device:TPU:0, one launch (start us, length us, event | category | flops | bytes accessed | tf_op | source)
XLA Modules:
  0.0 119.6 jit_solution(2477416987417581298)
XLA Ops:
  0.0 0.9 shard_map.73
  0.9 2.4 %collective-permute-start = (bf16[6,2048]{1,0:T(8,128)(2,1)S(1)}, bf16[6,2048]{1,0:T(8,128)(2,1)S(1)}, u32[]{:S(2)}, u32[]{:S(2)}) collective-permute-start(bf16[6,2048]{1,0:T(8,128)(2,1)S(1)} %shard_map.73), channel_id=1, source_target_pairs={{0,2},{2,4},{4,6},{6,8},{8,10},{10,12},{12,14},{14,16},{16,18},{18... | collective-permute-start | bytes 73736 | tf_op jit(solution)/shard_map/ppermute | solution.py:18
  3.4 4.8 %shard_map.74._ = bf16[16,640,128]{2,1,0:T(8,128)(2,1)} custom-call(f32[256,32,128]{2,1,0:T(8,128)} %bitcast.7), custom_call_target="tpu_custom_call" | custom-call | bytes 6291456 | tf_op jit(solution)/shard_map/pallas_call | solution.py:143
  8.2 1.6 %shard_map.75 = bf16[16,640,128]{2,1,0:T(8,128)(2,1)} custom-call(bf16[128,2048]{1,0:T(8,128)(2,1)S(1)} %copy-done, bf16[128,2048]{1,0:T(8,128)(2,1)S(1)} %copy-done.1, bf16[6,2048]{1,0:T(8,128)(2,1)S(1)} %collective-permute-done.tails_ref, f32[3,3,2048]{2,1,0:T(4,128)S(1)} %copy-done.6, ...), custom_call_target="tpu_custom_call", output_to_operand_aliasing={{}: (4, {})} | custom-call | flops 3145728 | bytes 1572864 | tf_op jit(solution)/shard_map/pallas_call | solution.py:171
  9.8 7.2 %all-to-all-start = ((bf16[16,640,128]{2,1,0:T(8,128)(2,1)}), bf16[16,640,128]{2,1,0:T(8,128)(2,1)S(1)}, u32[]{:S(2)}, u32[]{:S(2)}) async-start(bf16[16,640,128]{2,1,0:T(8,128)(2,1)} %shard_map.75), calls=%async_computation | async-start | bytes 5242880 | tf_op jit(solution)/shard_map/all_to_all | solution.py:535
  17.0 5.0 %shard_map.76 = (bf16[512,256]{1,0:T(8,128)(2,1)S(1)}, bf16[512,256]{1,0:T(8,128)(2,1)S(1)}, bf16[256,512]{1,0:T(8,128)(2,1)S(1)}, bf16[256,512]{1,0:T(8,128)(2,...) custom-call(), custom_call_target="tpu_custom_call" | custom-call | flops 52428800 | bytes 2097152 | tf_op jit(solution)/shard_map/pallas_call | solution.py:476
  22.0 1.0 copy-done.4
  23.0 1.0 copy-done.5
  24.0 0.7 copy-done.7
  24.7 0.7 copy-done.8
  25.4 0.7 copy-done.9
  26.1 0.7 copy-done.10
  26.8 40.3 %all-to-all-done.taken_ref = bf16[16,640,128]{2,1,0:T(8,128)(2,1)S(1)} async-done(((bf16[16,640,128]{2,1,0:T(8,128)(2,1)}), bf16[16,640,128]{2,1,0:T(8,128)(2,1)S(1)}, u32[]{:S(2)}, u32[]{:S(2)}) %all-to-all-start) | async-done | bytes 2621472 | tf_op jit(solution)/shard_map/all_to_all | solution.py:535
  67.1 5.9 %shard_map.77 = bf16[16,128,128]{2,1,0:T(8,128)(2,1)} custom-call(bf16[16,640,128]{2,1,0:T(8,128)(2,1)S(1)} %all-to-all-done.taken_ref, bf16[512,256]{1,0:T(8,128)(2,1)} %copy-done.7, bf16[512,256]{1,0:T(8,128)(2,1)} %copy-done.8, bf16[256,512]{1,0:T(8,128)(2,1)} %copy-done.9, bf16[256,512]{1,0:T(8,128)(2,1)} %copy-done.10, f32[8,256,128]{2,1,0:T(8,128)} %copy-done.4, ...), custom_call_target="tpu_custom_call" | custom-call | flops 1342177280 | bytes 2621440 | tf_op jit(solution)/shard_map/pallas_call | solution.py:495
  73.0 13.3 %all-to-all-start.1 = ((bf16[16,128,128]{2,1,0:T(8,128)(2,1)}), bf16[16,128,128]{2,1,0:T(8,128)(2,1)S(1)}, u32[]{:S(2)}, u32[]{:S(2)}) async-start(bf16[16,128,128]{2,1,0:T(8,128)(2,1)} %shard_map.77), calls=%async_computation.1 | async-start | bytes 1048576 | tf_op jit(solution)/shard_map/all_to_all | solution.py:539
  86.4 1.0 copy-done.2
  87.4 1.0 copy-done.3
  88.4 1.1 shard_map.78
  89.6 11.0 %all-to-all-done.1.conv_ref = bf16[16,128,128]{2,1,0:T(8,128)(2,1)S(1)} async-done(((bf16[16,128,128]{2,1,0:T(8,128)(2,1)}), bf16[16,128,128]{2,1,0:T(8,128)(2,1)S(1)}, u32[]{:S(2)}, u32[]{:S(2)}) %all-to-all-start.1) | async-done | bytes 524320 | tf_op jit(solution)/shard_map/all_to_all | solution.py:539
  100.6 4.0 %shard_map.79 = (bf16[128,2048]{1,0:T(8,128)(2,1)S(1)}, bf16[128,2048]{1,0:T(8,128)(2,1)S(1)}) custom-call(bf16[16,128,128]{2,1,0:T(8,128)(2,1)S(1)} %all-to-all-done.1.conv_ref, f32[128,2048]{1,0:T(8,128)S(1)} %get-tuple-element.21.gate_ref, f32[128,2048]{1,0:T(8,128)S(1)} %get-tuple-element.22.direct_ref, bf16[2048,4096]{1,0:T(8,128)(2,1)} %weight_ref.3), custom_call_target="tpu_custom_call" | custom-call | flops 1073741824 | bytes 8388608 | tf_op jit(solution)/shard_map/pallas_call | solution.py:268
  104.6 1.6 %collective-permute-start.1 = (bf16[128,2048]{1,0:T(8,128)(2,1)S(1)}, bf16[128,2048]{1,0:T(8,128)(2,1)S(1)}, u32[]{:S(2)}, u32[]{:S(2)}) collective-permute-start(bf16[128,2048]{1,0:T(8,128)(2,1)S(1)} %get-tuple-element.24), channel_id=1, source_target_pairs={{0,1},{1,0},{2,3},{3,2},{4,5},{5,4},{6,7},{7,6},{8,9},{9,8},{10,11... | collective-permute-start | bytes 1572872 | tf_op jit(solution)/shard_map/ppermute | solution.py:278
  106.2 4.0 %shard_map.80 = f32[128,2048]{1,0:T(8,128)S(1)} custom-call(bf16[128,2048]{1,0:T(8,128)(2,1)S(1)} %get-tuple-element.23.gated_ref, bf16[2048,4096]{1,0:T(8,128)(2,1)} %weight_ref.3), custom_call_target="tpu_custom_call" | custom-call | flops 1073741824 | bytes 8388608 | tf_op jit(solution)/shard_map/pallas_call | solution.py:279
  110.2 8.5 %collective-permute-done.1 = bf16[128,2048]{1,0:T(8,128)(2,1)S(1)} collective-permute-done((bf16[128,2048]{1,0:T(8,128)(2,1)S(1)}, bf16[128,2048]{1,0:T(8,128)(2,1)S(1)}, u32[]{:S(2)}, u32[]{:S(2)}) %collective-permute-start.1) | collective-permute-done | bytes 524320 | tf_op jit(solution)/shard_map/ppermute | solution.py:278
  118.7 0.9 add_convert_fusion
  (17 shorter events, 0.0 us)
Async XLA Ops:
  0.9 7.2 %collective-permute-start = (bf16[6,2048]{1,0:T(8,128)(2,1)S(1)}, bf16[6,2048]{1,0:T(8,128)(2,1)S(1)}, u32[]{:S(2)}, u32[]{:S(2)}) collective-permute-start(bf16[6,2048]{1,0:T(8,128)(2,1)S(1)} %shard_map.73), channel_id=1, source_target_pairs={{0,2},{2,4},{4,6},{6,8},{8,10},{10,12},{12,14},{14,16},{16,18},{18... | collective-permute-start | bytes 73736 | tf_op jit(solution)/shard_map/ppermute | solution.py:18
  3.3 4.8 %copy-start = (bf16[128,2048]{1,0:T(8,128)(2,1)S(1)}, bf16[128,2048]{1,0:T(8,128)(2,1)}, u32[]{:S(2)}) copy-start(bf16[128,2048]{1,0:T(8,128)(2,1)} %key_ref.5) | copy-start | bytes 1572868
  3.3 4.8 %copy-start.1 = (bf16[128,2048]{1,0:T(8,128)(2,1)S(1)}, bf16[128,2048]{1,0:T(8,128)(2,1)}, u32[]{:S(2)}) copy-start(bf16[128,2048]{1,0:T(8,128)(2,1)} %value_ref.5) | copy-start | bytes 1572868
  3.3 4.8 %copy-start.6 = (f32[3,3,2048]{2,1,0:T(4,128)S(1)}, f32[3,3,2048]{2,1,0:T(4,128)}, u32[]{:S(2)}) copy-start(f32[3,3,2048]{2,1,0:T(4,128)} %taps_ref.3) | copy-start | bytes 221188
  9.8 57.3 %all-to-all-start = ((bf16[16,640,128]{2,1,0:T(8,128)(2,1)}), bf16[16,640,128]{2,1,0:T(8,128)(2,1)S(1)}, u32[]{:S(2)}, u32[]{:S(2)}) async-start(bf16[16,640,128]{2,1,0:T(8,128)(2,1)} %shard_map.75), calls=%async_computation | async-start | bytes 5242880 | tf_op jit(solution)/shard_map/all_to_all | solution.py:535
  22.0 1.0 copy-start.4
  23.0 1.0 copy-start.5
  23.9 0.7 copy-start.7
  24.7 0.7 copy-start.8
  25.4 0.7 copy-start.9
  26.1 0.7 copy-start.10
  67.1 19.2 %copy-start.11 = (f32[2048]{0:T(1024)S(1)}, f32[2048]{0:T(1024)}, u32[]{:S(2)}) copy-start(f32[2048]{0:T(1024)} %param.11) | copy-start | bytes 24580
  73.0 27.6 %all-to-all-start.1 = ((bf16[16,128,128]{2,1,0:T(8,128)(2,1)}), bf16[16,128,128]{2,1,0:T(8,128)(2,1)S(1)}, u32[]{:S(2)}, u32[]{:S(2)}) async-start(bf16[16,128,128]{2,1,0:T(8,128)(2,1)} %shard_map.77), calls=%async_computation.1 | async-start | bytes 1048576 | tf_op jit(solution)/shard_map/all_to_all | solution.py:539
  86.4 1.0 copy-start.2
  87.4 1.0 copy-start.3
  104.6 14.0 %collective-permute-start.1 = (bf16[128,2048]{1,0:T(8,128)(2,1)S(1)}, bf16[128,2048]{1,0:T(8,128)(2,1)S(1)}, u32[]{:S(2)}, u32[]{:S(2)}) collective-permute-start(bf16[128,2048]{1,0:T(8,128)(2,1)S(1)} %get-tuple-element.24), channel_id=1, source_target_pairs={{0,1},{1,0},{2,3},{3,2},{4,5},{5,4},{6,7},{7,6},{8,9},{9,8},{10,11... | collective-permute-start | bytes 1572872 | tf_op jit(solution)/shard_map/ppermute | solution.py:278

commit v3 on v2

--- a/solution.py
+++ b/solution.py
@@ -1,3 +1,4 @@
+import functools
 import math
 
 import jax
@@ -118,15 +119,37 @@
     )(*(pltpu.with_memory_space_constraint(a, pltpu.HBM) for a in (query, key_in, value)))
 
 
-def pack_kernel(spectrum_ref, sent_ref, staged):
-    pairs, group, _ = spectrum_ref.shape
+def gather_rows(size, count, invert=False):
+    row = lax.broadcasted_iota(jnp.int32, (size, size), 0)
+    column = lax.broadcasted_iota(jnp.int32, (size, size), 1)
+    if invert:
+        row, column = column, row
+    inner = size // count
+    match = column == (row % inner) * count + row // inner
+    return jnp.where(match, 1.0, 0.0).astype(jnp.bfloat16)
+
+
+def exact_rows(matrix, left, right):
+    both = jnp.concatenate([left, right], axis=1)
+    return jnp.dot(matrix, both, preferred_element_type=jnp.float32).astype(jnp.bfloat16)
+
+
+def pack_kernel(spectrum_ref, sent_ref):
+    pairs, group, block = spectrum_ref.shape
     tokens = sent_ref.shape[1] - 2 * pairs
-    staged[...] = spectrum_ref[...].reshape(staged.shape)
-    for d in range(group // 2):
-        for r in range(2):
-            sent_ref[d, pl.ds(tokens + r * pairs, pairs), :] = staged[
-                pl.ds(2 * d + r, pairs, stride=group), :
-            ].astype(jnp.bfloat16)
+    part = pairs // group
+    matrix = gather_rows(pairs, group)
+    slabs = [
+        spectrum_ref[pl.ds(k * part, part)].reshape(pairs, block).astype(jnp.bfloat16)
+        for k in range(group)
+    ]
+    for k in range(0, group, 2):
+        both = exact_rows(matrix, slabs[k], slabs[k + 1])
+        for s in range(group):
+            rows = both[s * part : (s + 1) * part]
+            start = tokens + (s % 2) * pairs + k * part
+            sent_ref[s // 2, pl.ds(start, part), :] = rows[:, :block]
+            sent_ref[s // 2, pl.ds(start + part, part), :] = rows[:, block:]
 
 
 def packed_spectrum(filter_spectrum, devices):
@@ -146,7 +169,6 @@
         out_shape=jax.ShapeDtypeStruct((devices, rows, block), jnp.bfloat16),
         in_specs=[pl.BlockSpec((pairs, 8, block), lambda i: (0, i, 0))],
         out_specs=pl.BlockSpec((4, rows, block), lambda i: (i, 0, 0)),
-        scratch_shapes=[pltpu.VMEM((pairs * 8, block), jnp.float32)],
         compiler_params=pltpu.CompilerParams(vmem_limit_bytes=16 * 2**20),
         cost_estimate=pl.CostEstimate(
             flops=0, bytes_accessed=view.size * 6, transcendentals=0
@@ -208,11 +230,11 @@
     )(query, key_in, value, tails, short_taps, skip_gain[None, :])
 
 
-def chunk_copies(weight_ref, held, sems, rank):
+def chunk_copies(weight_ref, held, sems, first):
     chunks, _, width = held.shape
     return [
         pltpu.make_async_copy(
-            weight_ref.at[:, pl.ds(pl.multiple_of((rank * chunks + i) * width, width), width)],
+            weight_ref.at[:, pl.ds(pl.multiple_of((first + i) * width, width), width)],
             held.at[i],
             sems.at[i],
         )
@@ -220,9 +242,19 @@
     ]
 
 
+def multiply(gated_ref, share_ref, held, copies):
+    width = held.shape[2]
+    for i, copy in enumerate(copies):
+        copy.wait()
+        share_ref[:, pl.ds(i * width, width)] = jnp.dot(
+            gated_ref[...], held[i], preferred_element_type=jnp.float32
+        ).astype(share_ref.dtype)
+
+
 def far_kernel(conv_ref, gate_ref, direct_ref, weight_ref, gated_ref, share_ref, held, sems):
     devices, _, block = conv_ref.shape
-    copies = chunk_copies(weight_ref, held, sems, 1 - lax.axis_index("tp"))
+    chunks = weight_ref.shape[1] // 2 // WIDTH
+    copies = chunk_copies(weight_ref, held, sems, (1 - lax.axis_index("tp")) * chunks)
     for copy in copies:
         copy.start()
     for j in range(devices):
@@ -230,60 +262,64 @@
         gated_ref[:, lanes] = (
             gate_ref[:, lanes] * (conv_ref[j].astype(jnp.float32) + direct_ref[:, lanes])
         ).astype(jnp.bfloat16)
-    for i, copy in enumerate(copies):
-        copy.wait()
-        share_ref[:, pl.ds(i * WIDTH, WIDTH)] = jnp.dot(
-            gated_ref[...], held[i], preferred_element_type=jnp.float32
-        ).astype(jnp.bfloat16)
-
-
-def near_kernel(gated_ref, weight_ref, share_ref, held, sems):
-    copies = chunk_copies(weight_ref, held, sems, lax.axis_index("tp"))
+    multiply(gated_ref, share_ref, held, copies)
+
+
+def rest_kernel(far, gated_ref, weight_ref, share_ref, held, sems):
+    chunks = weight_ref.shape[1] // 2 // WIDTH
+    rank = lax.axis_index("tp")
+    first = (1 - rank) * chunks + chunks // 2 if far else rank * chunks
+    copies = chunk_copies(weight_ref, held, sems, first)
     for copy in copies:
         copy.start()
-    for i, copy in enumerate(copies):
-        copy.wait()
-        share_ref[:, pl.ds(i * WIDTH, WIDTH)] = jnp.dot(
-            gated_ref[...], held[i], preferred_element_type=jnp.float32
-        )
+    multiply(gated_ref, share_ref, held, copies)
 
 
 def projected(convolved, gate_signal, direct, out_weight):
     tokens, channels = gate_signal.shape
     columns = out_weight.shape[1] // 2
-    whole = pl.BlockSpec(memory_space=pltpu.VMEM)
-    cost = pl.CostEstimate(
-        flops=2 * tokens * channels * columns, bytes_accessed=2 * channels * columns, transcendentals=0
-    )
-    common = {
-        "scratch_shapes": [
-            pltpu.VMEM((columns // WIDTH, channels, WIDTH), jnp.bfloat16),
-            pltpu.SemaphoreType.DMA((columns // WIDTH,)),
-        ],
-        "compiler_params": pltpu.CompilerParams(vmem_limit_bytes=20 * 2**20),
-        "cost_estimate": cost,
-    }
+    whole, remote = pl.BlockSpec(memory_space=pltpu.VMEM), pl.BlockSpec(memory_space=pltpu.HBM)
     out_weight = pltpu.with_memory_space_constraint(out_weight, pltpu.HBM)
-    remote = pl.BlockSpec(memory_space=pltpu.HBM)
-    gated, far = pl.pallas_call(
+
+    def common(width):
+        return {
+            "scratch_shapes": [
+                pltpu.VMEM((width // WIDTH, channels, WIDTH), jnp.bfloat16),
+                pltpu.SemaphoreType.DMA((width // WIDTH,)),
+            ],
+            "compiler_params": pltpu.CompilerParams(vmem_limit_bytes=20 * 2**20),
+            "cost_estimate": pl.CostEstimate(
+                flops=2 * tokens * channels * width, bytes_accessed=2 * channels * width, transcendentals=0
+            ),
+        }
+
+    half = jax.ShapeDtypeStruct((tokens, columns // 2), jnp.bfloat16)
+    gated, far_one = pl.pallas_call(
         far_kernel,
-        out_shape=(
-            jax.ShapeDtypeStruct((tokens, channels), jnp.bfloat16),
-            jax.ShapeDtypeStruct((tokens, columns), jnp.bfloat16),
-        ),
+        out_shape=(jax.ShapeDtypeStruct((tokens, channels), jnp.bfloat16), half),
         in_specs=[whole] * 3 + [remote],
         out_specs=(whole, whole),
-        **common,
+        **common(columns // 2),
     )(convolved, gate_signal, direct, out_weight)
-    arrived = lax.ppermute(far, "tp", [(0, 1), (1, 0)])
+    swap = [(0, 1), (1, 0)]
+    arrived_one = lax.ppermute(far_one, "tp", swap)
+    far_two = pl.pallas_call(
+        functools.partial(rest_kernel, True),
+        out_shape=half,
+        in_specs=[whole, remote],
+        out_specs=whole,
+        **common(columns // 2),
+    )(gated, out_weight)
+    arrived_two = lax.ppermute(far_two, "tp", swap)
     near = pl.pallas_call(
-        near_kernel,
+        functools.partial(rest_kernel, False),
         out_shape=jax.ShapeDtypeStruct((tokens, columns), jnp.float32),
         in_specs=[whole, remote],
         out_specs=whole,
-        **common,
+        **common(columns),
     )(gated, out_weight)
-    return (near + arrived.astype(jnp.float32)).astype(jnp.bfloat16)
+    arrived = jnp.concatenate([arrived_one, arrived_two], axis=1).astype(jnp.float32)
+    return (near + arrived).astype(jnp.bfloat16)
 
 
 def butterfly(parts, sign):
@@ -323,7 +359,7 @@
     taken_ref, *refs,
 ):
     tables, out_ref = refs[:6], refs[6]
-    samples, packed, inner, flipped, high_ref, low_ref, done, sem = refs[7:15]
+    result_ref, packed, inner, flipped, high_ref, low_ref, done, sems = refs[7:15]
     held, table_sems = refs[15:21], refs[21]
     fwd_high, fwd_low, inv_high, inv_low, cos_ref, sin_ref = held
     loads = [pltpu.make_async_copy(*p, table_sems.at[i]) for i, p in enumerate(zip(tables, held))]
@@ -335,10 +371,17 @@
     lane = [pl.ds(v * block, block) for v in range(RADIX)]
     spectrum_real, spectrum_imag = pl.ds(tokens, half), pl.ds(tokens + half, half)
 
-    for q in range(devices):
-        samples[pl.ds(q * tokens, tokens), :] = taken_ref[q, pl.ds(0, tokens), :].astype(jnp.float32)
-    for v in range(RADIX):
-        packed[:, lane[v]] = samples[pl.ds(v, depth, stride=RADIX), :].astype(jnp.bfloat16)
+    part = half // RADIX
+    matrix = gather_rows(half, RADIX)
+    for k in range(0, RADIX, 2):
+        slabs = [taken_ref[2 * k + q, pl.ds(0, tokens), :] for q in range(4)]
+        both = exact_rows(
+            matrix, jnp.concatenate(slabs[:2], axis=0), jnp.concatenate(slabs[2:], axis=0)
+        )
+        for v in range(RADIX):
+            rows = both[v * part : (v + 1) * part]
+            packed[pl.ds(k * part, part), lane[v]] = rows[:, :block]
+            packed[pl.ds((k + 1) * part, part), lane[v]] = rows[:, block:]
 
     wide = 2 * block
     loads[0].wait()
@@ -424,13 +467,26 @@
             + jnp.dot(inv_low[...], right, preferred_element_type=jnp.float32)
             + jnp.dot(inv_high[...], low_ref[:, lanes], preferred_element_type=jnp.float32)
         ) * (0.5 / (devices * tokens))
-        samples[pl.ds(v, depth, stride=RADIX), :] = result[:, :block]
-        samples[pl.ds(v + 1, depth, stride=RADIX), :] = result[:, block:]
-    for q in range(devices):
-        done[q] = samples[pl.ds(q * tokens, tokens), :].astype(jnp.bfloat16)
-    copy = pltpu.make_async_copy(done, out_ref, sem)
-    copy.start()
-    copy.wait()
+        result_ref[:, lanes] = result.astype(jnp.bfloat16)
+
+    matrix = gather_rows(half, RADIX, invert=True)
+    copies = []
+    for k in range(0, RADIX, 2):
+        slabs = [
+            jnp.concatenate([result_ref[pl.ds(p * part, part), lane[v]] for v in range(RADIX)], axis=0)
+            for p in (k, k + 1)
+        ]
+        both = exact_rows(matrix, *slabs)
+        for q in range(4):
+            done[2 * k + q] = both[(q % 2) * tokens : (q % 2 + 1) * tokens, (q // 2) * block : (q // 2 + 1) * block]
+        copies.append(
+            pltpu.make_async_copy(
+                done.at[pl.ds(2 * k, 4)], out_ref.at[pl.ds(2 * k, 4)], sems.at[k // 2]
+            )
+        )
+        copies[-1].start()
+    for copy in copies:
+        copy.wait()
 
 
 def angles_of(shape, rows, columns, order):
@@ -498,14 +554,14 @@
         in_specs=[whole] + [remote] * 6,
         out_specs=remote,
         scratch_shapes=[
-            pltpu.VMEM((length, block), jnp.float32),
+            pltpu.VMEM((depth, wide), jnp.bfloat16),
             pltpu.VMEM((depth, wide), jnp.bfloat16),
             pltpu.VMEM((2 * half, wide), jnp.float32),
             pltpu.VMEM((RADIX, half, 2 * block), jnp.bfloat16),
             pltpu.VMEM((2 * half, wide), jnp.bfloat16),
             pltpu.VMEM((2 * half, wide), jnp.bfloat16),
             pltpu.VMEM((devices, tokens, block), jnp.bfloat16),
-            pltpu.SemaphoreType.DMA,
+            pltpu.SemaphoreType.DMA((RADIX // 2,)),
             *(pltpu.VMEM(t.shape, t.dtype) for t in tables),
             pltpu.SemaphoreType.DMA((len(tables),)),
         ],

time: 120 us -> 122 us (1.017)
  Pallas kernels: 27.3 us -> 28.9 us
    pallas_call x1 -> x2, Pallas kernels: 4 us -> 6.72 us  [the longest x1 4 us: projected(): pl.pallas_call(functools.partial(rest_kernel, False), out_shape=jax.Shape...]
    pallas_call x1, Pallas kernels: 4.02 us -> 2.73 us  [projected(): pl.pallas_call(far_kernel, out_shape=(jax.ShapeDtypeStruct((tokens, chann...]
    ppermute x1 -> x2, waiting for transfers between devices: 8.48 us -> 7.94 us  [the longest x1 4.79 us: projected(): arrived_one = lax.ppermute(far_one, 'tp', swap)]
  transfers between devices with their start and end apart: 4 -> 5, of which waited for: 3 -> 4; matrix products, arithmetic and copies ran while one was open for 0% -> 0% of each run, Pallas kernels for 12% -> 12%
where the time goes in v3:
time: 122 us; the launch traced here: 121 us
  waiting for transfers between devices  59.3 us (49%)
  Pallas kernels  28.9 us (24%)
  starting transfers between devices  25 us (20%)
  local copies, waits for them, and re-layouts  6.85 us (6%)
    all_to_all x1, waiting for transfers between devices, fused_shards(): taken = lax.all_to_all(sent, 'ctx', split_axis=0, concat_axis=0, tiled=True)  40.3 us
    all_to_all x1, starting transfers between devices, fused_shards(): lax.all_to_all(convolved, 'ctx', split_axis=0, concat_axis=0, tiled=True)  13.3 us
    all_to_all x1, waiting for transfers between devices, fused_shards(): lax.all_to_all(convolved, 'ctx', split_axis=0, concat_axis=0, tiled=True)  11 us
    all_to_all x1, starting transfers between devices, fused_shards(): taken = lax.all_to_all(sent, 'ctx', split_axis=0, concat_axis=0, tiled=True)  7.21 us
    unnamed x24, local copies, waits for them, and re-layouts  6.85 us
    pallas_call x1, Pallas kernels, local_transform(): pl.pallas_call(transform_kernel, out_shape=pltpu.HBM((devices, tokens, bl...  5.97 us
    pallas_call x1, Pallas kernels, local_tables(): pl.pallas_call(tables_kernel, out_shape=(forward, forward, inverse, inver...  4.99 us
    pallas_call x1, Pallas kernels, packed_spectrum(): pl.pallas_call(pack_kernel, grid=(devices // 4,), out_shape=jax.ShapeDtyp...  4.93 us
  transfers between devices with their start and end apart: 5, of which 4 were waited for; matrix products, arithmetic and copies ran while one was open for 0% of the time, Pallas kernels for 12%

profile of v3, /device:TPU:0, one launch (start us, length us, event | category | flops | bytes accessed | tf_op | source)
XLA Modules:
  0.0 121.2 jit_solution(15990343187771754746)
XLA Ops:
  0.0 0.9 shard_map.73
  0.9 2.4 %collective-permute-start = (bf16[6,2048]{1,0:T(8,128)(2,1)S(1)}, bf16[6,2048]{1,0:T(8,128)(2,1)S(1)}, u32[]{:S(2)}, u32[]{:S(2)}) collective-permute-start(bf16[6,2048]{1,0:T(8,128)(2,1)S(1)} %shard_map.73), channel_id=1, source_target_pairs={{0,2},{2,4},{4,6},{6,8},{8,10},{10,12},{12,14},{14,16},{16,18},{18... | collective-permute-start | bytes 73736 | tf_op jit(solution)/shard_map/ppermute | solution.py:19
  3.4 4.9 %shard_map.74._ = bf16[16,640,128]{2,1,0:T(8,128)(2,1)} custom-call(f32[256,32,128]{2,1,0:T(8,128)} %bitcast.7), custom_call_target="tpu_custom_call" | custom-call | bytes 6291456 | tf_op jit(solution)/shard_map/pallas_call | solution.py:166
  8.3 1.6 %shard_map.75 = bf16[16,640,128]{2,1,0:T(8,128)(2,1)} custom-call(bf16[128,2048]{1,0:T(8,128)(2,1)S(1)} %copy-done, bf16[128,2048]{1,0:T(8,128)(2,1)S(1)} %copy-done.1, bf16[6,2048]{1,0:T(8,128)(2,1)S(1)} %collective-permute-done.tails_ref, f32[3,3,2048]{2,1,0:T(4,128)S(1)} %copy-done.6, ...), custom_call_target="tpu_custom_call", output_to_operand_aliasing={{}: (4, {})} | custom-call | flops 3145728 | bytes 1572864 | tf_op jit(solution)/shard_map/pallas_call | solution.py:193
  9.9 7.2 %all-to-all-start = ((bf16[16,640,128]{2,1,0:T(8,128)(2,1)}), bf16[16,640,128]{2,1,0:T(8,128)(2,1)S(1)}, u32[]{:S(2)}, u32[]{:S(2)}) async-start(bf16[16,640,128]{2,1,0:T(8,128)(2,1)} %shard_map.75), calls=%async_computation | async-start | bytes 5242880 | tf_op jit(solution)/shard_map/all_to_all | solution.py:591
  17.1 5.0 %shard_map.76 = (bf16[512,256]{1,0:T(8,128)(2,1)S(1)}, bf16[512,256]{1,0:T(8,128)(2,1)S(1)}, bf16[256,512]{1,0:T(8,128)(2,1)S(1)}, bf16[256,512]{1,0:T(8,128)(2,...) custom-call(), custom_call_target="tpu_custom_call" | custom-call | flops 52428800 | bytes 2097152 | tf_op jit(solution)/shard_map/pallas_call | solution.py:532
  22.1 1.0 copy-done.4
  23.0 1.0 copy-done.5
  24.0 0.7 copy-done.7
  25.4 0.7 copy-done.9
  26.8 40.3 %all-to-all-done.taken_ref = bf16[16,640,128]{2,1,0:T(8,128)(2,1)S(1)} async-done(((bf16[16,640,128]{2,1,0:T(8,128)(2,1)}), bf16[16,640,128]{2,1,0:T(8,128)(2,1)S(1)}, u32[]{:S(2)}, u32[]{:S(2)}) %all-to-all-start) | async-done | bytes 2621472 | tf_op jit(solution)/shard_map/all_to_all | solution.py:591
  67.2 6.0 %shard_map.77 = bf16[16,128,128]{2,1,0:T(8,128)(2,1)} custom-call(bf16[16,640,128]{2,1,0:T(8,128)(2,1)S(1)} %all-to-all-done.taken_ref, bf16[512,256]{1,0:T(8,128)(2,1)} %copy-done.7, bf16[512,256]{1,0:T(8,128)(2,1)} %copy-done.8, bf16[256,512]{1,0:T(8,128)(2,1)} %copy-done.9, bf16[256,512]{1,0:T(8,128)(2,1)} %copy-done.10, f32[8,256,128]{2,1,0:T(8,128)} %copy-done.4, ...), custom_call_target="tpu_custom_call" | custom-call | flops 1342177280 | bytes 2621440 | tf_op jit(solution)/shard_map/pallas_call | solution.py:551
  73.2 13.3 %all-to-all-start.1 = ((bf16[16,128,128]{2,1,0:T(8,128)(2,1)}), bf16[16,128,128]{2,1,0:T(8,128)(2,1)S(1)}, u32[]{:S(2)}, u32[]{:S(2)}) async-start(bf16[16,128,128]{2,1,0:T(8,128)(2,1)} %shard_map.77), calls=%async_computation.1 | async-start | bytes 1048576 | tf_op jit(solution)/shard_map/all_to_all | solution.py:595
  86.5 1.0 copy-done.2
  87.6 1.0 copy-done.3
  88.6 1.1 shard_map.78
  89.7 11.0 %all-to-all-done.1.conv_ref = bf16[16,128,128]{2,1,0:T(8,128)(2,1)S(1)} async-done(((bf16[16,128,128]{2,1,0:T(8,128)(2,1)}), bf16[16,128,128]{2,1,0:T(8,128)(2,1)S(1)}, u32[]{:S(2)}, u32[]{:S(2)}) %all-to-all-start.1) | async-done | bytes 524320 | tf_op jit(solution)/shard_map/all_to_all | solution.py:595
  100.8 2.7 %shard_map.79 = (bf16[128,2048]{1,0:T(8,128)(2,1)S(1)}, bf16[128,1024]{1,0:T(8,128)(2,1)S(1)}) custom-call(bf16[16,128,128]{2,1,0:T(8,128)(2,1)S(1)} %all-to-all-done.1.conv_ref, f32[128,2048]{1,0:T(8,128)S(1)} %get-tuple-element.21.gate_ref, f32[128,2048]{1,0:T(8,128)S(1)} %get-tuple-element.22.direct_ref, bf16[2048,4096]{1,0:T(8,128)(2,1)} %weight_ref.5), custom_call_target="tpu_custom_call" | custom-call | flops 536870912 | bytes 4194304 | tf_op jit(solution)/shard_map/pallas_call | solution.py:297
  103.5 2.7 %shard_map.81 = bf16[128,1024]{1,0:T(8,128)(2,1)S(1)} custom-call(bf16[128,2048]{1,0:T(8,128)(2,1)S(1)} %get-tuple-element.23.gated_ref, bf16[2048,4096]{1,0:T(8,128)(2,1)} %weight_ref.5), custom_call_target="tpu_custom_call" | custom-call | flops 536870912 | bytes 4194304 | tf_op jit(solution)/shard_map/pallas_call | solution.py:306
  106.2 1.5 %collective-permute-start.2 = (bf16[128,1024]{1,0:T(8,128)(2,1)S(1)}, bf16[128,1024]{1,0:T(8,128)(2,1)S(1)}, u32[]{:S(2)}, u32[]{:S(2)}) collective-permute-start(bf16[128,1024]{1,0:T(8,128)(2,1)S(1)} %shard_map.81), channel_id=1, source_target_pairs={{0,1},{1,0},{2,3},{3,2},{4,5},{5,4},{6,7},{7,6},{8,9},{9,8},{10,11... | collective-permute-start | bytes 786440 | tf_op jit(solution)/shard_map/ppermute | solution.py:313
  108.3 4.0 %shard_map.80 = f32[128,2048]{1,0:T(8,128)S(1)} custom-call(bf16[128,2048]{1,0:T(8,128)(2,1)S(1)} %get-tuple-element.23.gated_ref, bf16[2048,4096]{1,0:T(8,128)(2,1)} %weight_ref.5), custom_call_target="tpu_custom_call" | custom-call | flops 1073741824 | bytes 8388608 | tf_op jit(solution)/shard_map/pallas_call | solution.py:314
  112.3 3.1 %collective-permute-done.2 = bf16[128,1024]{1,0:T(8,128)(2,1)S(1)} collective-permute-done((bf16[128,1024]{1,0:T(8,128)(2,1)S(1)}, bf16[128,1024]{1,0:T(8,128)(2,1)S(1)}, u32[]{:S(2)}, u32[]{:S(2)}) %collective-permute-start.2) | collective-permute-done | bytes 262176 | tf_op jit(solution)/shard_map/ppermute | solution.py:313
  115.5 4.8 %collective-permute-done.1 = bf16[128,1024]{1,0:T(8,128)(2,1)S(1)} collective-permute-done((bf16[128,1024]{1,0:T(8,128)(2,1)S(1)}, bf16[128,1024]{1,0:T(8,128)(2,1)S(1)}, u32[]{:S(2)}, u32[]{:S(2)}) %collective-permute-start.1) | collective-permute-done | bytes 262176 | tf_op jit(solution)/shard_map/ppermute | solution.py:305
  120.3 0.9 add_convert_fusion
  (20 shorter events, 2.0 us)
Async XLA Ops:
  0.9 7.4 %collective-permute-start = (bf16[6,2048]{1,0:T(8,128)(2,1)S(1)}, bf16[6,2048]{1,0:T(8,128)(2,1)S(1)}, u32[]{:S(2)}, u32[]{:S(2)}) collective-permute-start(bf16[6,2048]{1,0:T(8,128)(2,1)S(1)} %shard_map.73), channel_id=1, source_target_pairs={{0,2},{2,4},{4,6},{6,8},{8,10},{10,12},{12,14},{14,16},{16,18},{18... | collective-permute-start | bytes 73736 | tf_op jit(solution)/shard_map/ppermute | solution.py:19
  3.3 5.0 %copy-start = (bf16[128,2048]{1,0:T(8,128)(2,1)S(1)}, bf16[128,2048]{1,0:T(8,128)(2,1)}, u32[]{:S(2)}) copy-start(bf16[128,2048]{1,0:T(8,128)(2,1)} %key_ref.5) | copy-start | bytes 1572868
  3.3 5.0 %copy-start.1 = (bf16[128,2048]{1,0:T(8,128)(2,1)S(1)}, bf16[128,2048]{1,0:T(8,128)(2,1)}, u32[]{:S(2)}) copy-start(bf16[128,2048]{1,0:T(8,128)(2,1)} %value_ref.5) | copy-start | bytes 1572868
  3.3 5.0 %copy-start.6 = (f32[3,3,2048]{2,1,0:T(4,128)S(1)}, f32[3,3,2048]{2,1,0:T(4,128)}, u32[]{:S(2)}) copy-start(f32[3,3,2048]{2,1,0:T(4,128)} %taps_ref.3) | copy-start | bytes 221188
  9.9 57.3 %all-to-all-start = ((bf16[16,640,128]{2,1,0:T(8,128)(2,1)}), bf16[16,640,128]{2,1,0:T(8,128)(2,1)S(1)}, u32[]{:S(2)}, u32[]{:S(2)}) async-start(bf16[16,640,128]{2,1,0:T(8,128)(2,1)} %shard_map.75), calls=%async_computation | async-start | bytes 5242880 | tf_op jit(solution)/shard_map/all_to_all | solution.py:591
  22.1 1.0 copy-start.4
  23.0 1.0 copy-start.5
  24.0 0.7 copy-start.7
  24.7 0.7 copy-start.8
  25.4 0.7 copy-start.9
  26.1 0.7 copy-start.10
  67.2 19.3 %copy-start.11 = (f32[2048]{0:T(1024)S(1)}, f32[2048]{0:T(1024)}, u32[]{:S(2)}) copy-start(f32[2048]{0:T(1024)} %param.11) | copy-start | bytes 24580
  73.2 27.6 %all-to-all-start.1 = ((bf16[16,128,128]{2,1,0:T(8,128)(2,1)}), bf16[16,128,128]{2,1,0:T(8,128)(2,1)S(1)}, u32[]{:S(2)}, u32[]{:S(2)}) async-start(bf16[16,128,128]{2,1,0:T(8,128)(2,1)} %shard_map.77), calls=%async_computation.1 | async-start | bytes 1048576 | tf_op jit(solution)/shard_map/all_to_all | solution.py:595
  86.5 1.0 copy-start.2
  87.6 1.0 copy-start.3
  106.2 9.2 %collective-permute-start.2 = (bf16[128,1024]{1,0:T(8,128)(2,1)S(1)}, bf16[128,1024]{1,0:T(8,128)(2,1)S(1)}, u32[]{:S(2)}, u32[]{:S(2)}) collective-permute-start(bf16[128,1024]{1,0:T(8,128)(2,1)S(1)} %shard_map.81), channel_id=1, source_target_pairs={{0,1},{1,0},{2,3},{3,2},{4,5},{5,4},{6,7},{7,6},{8,9},{9,8},{10,11... | collective-permute-start | bytes 786440 | tf_op jit(solution)/shard_map/ppermute | solution.py:313
  107.8 12.5 %collective-permute-start.1 = (bf16[128,1024]{1,0:T(8,128)(2,1)S(1)}, bf16[128,1024]{1,0:T(8,128)(2,1)S(1)}, u32[]{:S(2)}, u32[]{:S(2)}) collective-permute-start(bf16[128,1024]{1,0:T(8,128)(2,1)S(1)} %get-tuple-element.24), channel_id=1, source_target_pairs={{0,1},{1,0},{2,3},{3,2},{4,5},{5,4},{6,7},{7,6},{8,9},{9,8},{10,11... | collective-permute-start | bytes 786440 | tf_op jit(solution)/shard_map/ppermute | solution.py:305

commit v4 on v3

--- a/solution.py
+++ b/solution.py
@@ -8,10 +8,14 @@
 from jax.experimental.pallas import tpu as pltpu
 from jax.sharding import PartitionSpec as P
 
+
 RADIX = 8
 ROWS = 16
 LANES = 128
-WIDTH = 512
+FAR_CHUNKS = (512, 512, 1024)
+NEAR_WIDTH = 512
+GROUP = 64
+EDGE = 8
 
 
 def shifted_in(rows, axis):
@@ -84,11 +88,6 @@
     return high, (value - high.astype(jnp.float32)).astype(jnp.bfloat16)
 
 
-def split_table(value):
-    high = lax.reduce_precision(value, exponent_bits=8, mantissa_bits=7)
-    return high.astype(jnp.bfloat16), (value - high).astype(jnp.bfloat16)
-
-
 def filtered_block(signal_ref, tails_ref, taps_ref, which, lanes):
     values = signal_ref[:, lanes].astype(jnp.float32)
     tails = tails_ref[:, lanes].astype(jnp.float32)
@@ -134,78 +133,97 @@
     return jnp.dot(matrix, both, preferred_element_type=jnp.float32).astype(jnp.bfloat16)
 
 
-def pack_kernel(spectrum_ref, sent_ref):
-    pairs, group, block = spectrum_ref.shape
-    tokens = sent_ref.shape[1] - 2 * pairs
-    part = pairs // group
-    matrix = gather_rows(pairs, group)
-    slabs = [
-        spectrum_ref[pl.ds(k * part, part)].reshape(pairs, block).astype(jnp.bfloat16)
-        for k in range(group)
+def unshifted(values, taps):
+    return taps[0:1] * values + taps[1:2] * pltpu.roll(values, 1, 0) + taps[2:3] * pltpu.roll(values, 2, 0)
+
+
+def prepare_kernel(spectrum_ref, key_ref, value_ref, taps_ref, sent_ref, *scratch):
+    spectrum, key, value, taps, staged, in_sems, out_sems = scratch
+    devices, _, block = staged.shape
+    tokens = key.shape[0]
+    fine = 2 * devices
+    slab = GROUP * fine
+    groups = spectrum.shape[0] // slab
+    loads = [
+        pltpu.make_async_copy(source, target, in_sems.at[i])
+        for i, (source, target) in enumerate(((taps_ref, taps), (key_ref, key), (value_ref, value)))
+    ] + [
+        pltpu.make_async_copy(
+            spectrum_ref.at[pl.ds(g * slab, slab)], spectrum.at[pl.ds(g * slab, slab)], in_sems.at[3 + g]
+        )
+        for g in range(groups)
     ]
-    for k in range(0, group, 2):
-        both = exact_rows(matrix, slabs[k], slabs[k + 1])
-        for s in range(group):
-            rows = both[s * part : (s + 1) * part]
-            start = tokens + (s % 2) * pairs + k * part
-            sent_ref[s // 2, pl.ds(start, part), :] = rows[:, :block]
-            sent_ref[s // 2, pl.ds(start + part, part), :] = rows[:, block:]
-
-
-def packed_spectrum(filter_spectrum, devices):
+    for load in loads:
+        load.start()
+    stores = []
+
+    def store(start, size):
+        rows = pl.ds(start, size)
+        stores.append(
+            pltpu.make_async_copy(staged.at[:, rows], sent_ref.at[:, rows], out_sems.at[len(stores)])
+        )
+        stores[-1].start()
+
+    for load in loads[:3]:
+        load.wait()
+    edge = tokens + 2 * GROUP * groups
+    for j in range(devices):
+        lanes = pl.ds(j * block, block)
+        k, v = key[:, lanes].astype(jnp.float32), value[:, lanes].astype(jnp.float32)
+        mixed = unshifted(k, taps[1, :, lanes]) * unshifted(v, taps[2, :, lanes])
+        staged[j, pl.ds(0, tokens), :] = mixed.astype(jnp.bfloat16)
+        ends = jnp.concatenate([k[:2], v[:2], k[tokens - 2 :], v[tokens - 2 :]], axis=0)
+        staged[j, pl.ds(edge, EDGE), :] = ends.astype(jnp.bfloat16)
+    store(0, tokens)
+    store(edge, EDGE)
+
+    for g in range(groups):
+        loads[3 + g].wait()
+        start = tokens + 2 * GROUP * g
+        for s in range(fine):
+            staged[s // 2, pl.ds(start + s % 2 * GROUP, GROUP), :] = spectrum[
+                pl.ds(g * GROUP * fine + s, GROUP, stride=fine), :
+            ].astype(jnp.bfloat16)
+        store(start, 2 * GROUP)
+    for copy in stores:
+        copy.wait()
+
+
+def prepared(key_in, value, short_taps, filter_spectrum, devices):
     tokens, _, _, channels = filter_spectrum.shape
-    block = channels // devices
-    pairs = 2 * tokens
+    block, pairs = channels // devices, 2 * tokens
+    groups = pairs // GROUP
     view = (
         filter_spectrum.reshape(tokens, 2, 2, devices, block)
         .transpose(0, 1, 3, 2, 4)
-        .reshape(pairs, 2 * devices, block)
-    )
-    rows = tokens + 2 * pairs
-    view = pltpu.with_memory_space_constraint(view, pltpu.HBM)
+        .reshape(2 * pairs * devices, block)
+    )
+    rows = tokens + 2 * pairs + EDGE
+    remote = pl.BlockSpec(memory_space=pltpu.HBM)
+    inputs = [
+        pltpu.with_memory_space_constraint(a, pltpu.HBM) for a in (view, key_in, value, short_taps)
+    ]
     return pl.pallas_call(
-        pack_kernel,
-        grid=(devices // 4,),
-        out_shape=jax.ShapeDtypeStruct((devices, rows, block), jnp.bfloat16),
-        in_specs=[pl.BlockSpec((pairs, 8, block), lambda i: (0, i, 0))],
-        out_specs=pl.BlockSpec((4, rows, block), lambda i: (i, 0, 0)),
-        compiler_params=pltpu.CompilerParams(vmem_limit_bytes=16 * 2**20),
-        cost_estimate=pl.CostEstimate(
-            flops=0, bytes_accessed=view.size * 6, transcendentals=0
-        ),
-    )(view)
-
-
-def mix_kernel(key_ref, value_ref, tails_ref, taps_ref, _, sent_ref):
-    devices, _, block = sent_ref.shape
-    for j in range(devices):
-        lanes = pl.ds(j * block, block)
-        mixed = filtered_block(key_ref, tails_ref, taps_ref, 1, lanes) * filtered_block(
-            value_ref, tails_ref, taps_ref, 2, lanes
-        )
-        sent_ref[j] = mixed.astype(jnp.bfloat16)
-
-
-def with_signal(key_in, value, tails, short_taps, sent):
-    devices, _, block = sent.shape
-    tokens = key_in.shape[0]
-    whole = pl.BlockSpec(memory_space=pltpu.VMEM)
-    return pl.pallas_call(
-        mix_kernel,
-        grid=(1,),
-        out_shape=jax.ShapeDtypeStruct(sent.shape, sent.dtype),
-        in_specs=[whole] * 4 + [pl.BlockSpec(memory_space=pl.ANY)],
-        out_specs=pl.BlockSpec((devices, tokens, block), lambda i: (0, 0, 0)),
-        input_output_aliases={4: 0},
-        compiler_params=pltpu.CompilerParams(vmem_limit_bytes=16 * 2**20),
-        cost_estimate=pl.CostEstimate(
-            flops=12 * key_in.size, bytes_accessed=6 * key_in.size, transcendentals=0
-        ),
-    )(key_in, value, tails, short_taps, sent)
+        prepare_kernel,
+        out_shape=pltpu.HBM((devices, rows, block), jnp.bfloat16),
+        in_specs=[remote] * 4,
+        out_specs=remote,
+        scratch_shapes=[
+            pltpu.VMEM(view.shape, jnp.float32),
+            pltpu.VMEM((tokens, channels), jnp.bfloat16),
+            pltpu.VMEM((tokens, channels), jnp.bfloat16),
+            pltpu.VMEM(short_taps.shape, jnp.float32),
+            pltpu.VMEM((devices, rows, block), jnp.bfloat16),
+            pltpu.SemaphoreType.DMA((3 + groups,)),
+            pltpu.SemaphoreType.DMA((2 + groups,)),
+        ],
+        compiler_params=pltpu.CompilerParams(vmem_limit_bytes=20 * 2**20),
+        cost_estimate=pl.CostEstimate(flops=0, bytes_accessed=view.size * 6, transcendentals=0),
+    )(*inputs)
 
 
 def gate_kernel(query_ref, key_ref, value_ref, tails_ref, taps_ref, gain_ref, gate_ref, direct_ref):
-    tokens, channels = query_ref.shape
+    _, channels = query_ref.shape
     for j in range(channels // LANES):
         lanes = pl.ds(j * LANES, LANES)
         mixed = filtered_block(key_ref, tails_ref, taps_ref, 1, lanes) * filtered_block(
@@ -230,11 +248,11 @@
     )(query, key_in, value, tails, short_taps, skip_gain[None, :])
 
 
-def chunk_copies(weight_ref, held, sems, first):
+def column_copies(weight_ref, held, sems, first):
     chunks, _, width = held.shape
     return [
         pltpu.make_async_copy(
-            weight_ref.at[:, pl.ds(pl.multiple_of((first + i) * width, width), width)],
+            weight_ref.at[:, pl.ds(pl.multiple_of(first + i * width, LANES), width)],
             held.at[i],
             sems.at[i],
         )
@@ -251,10 +269,10 @@
         ).astype(share_ref.dtype)
 
 
-def far_kernel(conv_ref, gate_ref, direct_ref, weight_ref, gated_ref, share_ref, held, sems):
+def gated_kernel(conv_ref, gate_ref, direct_ref, weight_ref, gated_ref, share_ref, held, sems):
     devices, _, block = conv_ref.shape
-    chunks = weight_ref.shape[1] // 2 // WIDTH
-    copies = chunk_copies(weight_ref, held, sems, (1 - lax.axis_index("tp")) * chunks)
+    columns = weight_ref.shape[1] // 2
+    copies = column_copies(weight_ref, held, sems, (1 - lax.axis_index("tp")) * columns)
     for copy in copies:
         copy.start()
     for j in range(devices):
@@ -265,11 +283,10 @@
     multiply(gated_ref, share_ref, held, copies)
 
 
-def rest_kernel(far, gated_ref, weight_ref, share_ref, held, sems):
-    chunks = weight_ref.shape[1] // 2 // WIDTH
+def share_kernel(far, offset, gated_ref, weight_ref, share_ref, held, sems):
+    columns = weight_ref.shape[1] // 2
     rank = lax.axis_index("tp")
-    first = (1 - rank) * chunks + chunks // 2 if far else rank * chunks
-    copies = chunk_copies(weight_ref, held, sems, first)
+    copies = column_copies(weight_ref, held, sems, (1 - rank if far else rank) * columns + offset)
     for copy in copies:
         copy.start()
     multiply(gated_ref, share_ref, held, copies)
@@ -281,45 +298,43 @@
     whole, remote = pl.BlockSpec(memory_space=pltpu.VMEM), pl.BlockSpec(memory_space=pltpu.HBM)
     out_weight = pltpu.with_memory_space_constraint(out_weight, pltpu.HBM)
 
-    def common(width):
-        return {
-            "scratch_shapes": [
-                pltpu.VMEM((width // WIDTH, channels, WIDTH), jnp.bfloat16),
-                pltpu.SemaphoreType.DMA((width // WIDTH,)),
+    def share(kernel, operands, extra, width, step, dtype):
+        return pl.pallas_call(
+            kernel,
+            out_shape=(*extra, jax.ShapeDtypeStruct((tokens, width), dtype)),
+            in_specs=[whole] * len(operands) + [remote],
+            out_specs=(whole,) * (len(extra) + 1),
+            scratch_shapes=[
+                pltpu.VMEM((width // step, channels, step), jnp.bfloat16),
+                pltpu.SemaphoreType.DMA((width // step,)),
             ],
-            "compiler_params": pltpu.CompilerParams(vmem_limit_bytes=20 * 2**20),
-            "cost_estimate": pl.CostEstimate(
+            compiler_params=pltpu.CompilerParams(vmem_limit_bytes=20 * 2**20),
+            cost_estimate=pl.CostEstimate(
                 flops=2 * tokens * channels * width, bytes_accessed=2 * channels * width, transcendentals=0
             ),
-        }
-
-    half = jax.ShapeDtypeStruct((tokens, columns // 2), jnp.bfloat16)
-    gated, far_one = pl.pallas_call(
-        far_kernel,
-        out_shape=(jax.ShapeDtypeStruct((tokens, channels), jnp.bfloat16), half),
-        in_specs=[whole] * 3 + [remote],
-        out_specs=(whole, whole),
-        **common(columns // 2),
-    )(convolved, gate_signal, direct, out_weight)
+        )(*operands, out_weight)
+
     swap = [(0, 1), (1, 0)]
-    arrived_one = lax.ppermute(far_one, "tp", swap)
-    far_two = pl.pallas_call(
-        functools.partial(rest_kernel, True),
-        out_shape=half,
-        in_specs=[whole, remote],
-        out_specs=whole,
-        **common(columns // 2),
-    )(gated, out_weight)
-    arrived_two = lax.ppermute(far_two, "tp", swap)
-    near = pl.pallas_call(
-        functools.partial(rest_kernel, False),
-        out_shape=jax.ShapeDtypeStruct((tokens, columns), jnp.float32),
-        in_specs=[whole, remote],
-        out_specs=whole,
-        **common(columns),
-    )(gated, out_weight)
-    arrived = jnp.concatenate([arrived_one, arrived_two], axis=1).astype(jnp.float32)
-    return (near + arrived).astype(jnp.bfloat16)
+    widths = FAR_CHUNKS if sum(FAR_CHUNKS) == columns else (columns,)
+    arrived, offset, gated = [], 0, None
+    for width in widths:
+        if gated is None:
+            gated, far = share(
+                gated_kernel,
+                (convolved, gate_signal, direct),
+                (jax.ShapeDtypeStruct((tokens, channels), jnp.bfloat16),),
+                width,
+                min(width, NEAR_WIDTH),
+                jnp.bfloat16,
+            )
+        else:
+            kernel = functools.partial(share_kernel, True, offset)
+            (far,) = share(kernel, (gated,), (), width, min(width, NEAR_WIDTH), jnp.bfloat16)
+        arrived.append(lax.ppermute(far, "tp", swap))
+        offset += width
+    kernel = functools.partial(share_kernel, False, 0)
+    (near,) = share(kernel, (gated,), (), columns, NEAR_WIDTH, jnp.float32)
+    return (near + jnp.concatenate(arrived, axis=1).astype(jnp.float32)).astype(jnp.bfloat16)
 
 
 def butterfly(parts, sign):
@@ -356,25 +371,55 @@
 
 
 def transform_kernel(
-    taken_ref, *refs,
+    taken_ref, taps_ref, *refs,
 ):
     tables, out_ref = refs[:6], refs[6]
     result_ref, packed, inner, flipped, high_ref, low_ref, done, sems = refs[7:15]
-    held, table_sems = refs[15:21], refs[21]
+    held, table_sems, edges = refs[15:21], refs[21], refs[22]
     fwd_high, fwd_low, inv_high, inv_low, cos_ref, sin_ref = held
     loads = [pltpu.make_async_copy(*p, table_sems.at[i]) for i, p in enumerate(zip(tables, held))]
     for load in loads:
         load.start()
     devices, tokens, block = done.shape
-    depth = packed.shape[0]
     half = cos_ref.shape[1]
     lane = [pl.ds(v * block, block) for v in range(RADIX)]
-    spectrum_real, spectrum_imag = pl.ds(tokens, half), pl.ds(tokens + half, half)
+    edge = tokens + 2 * half
+
+    edges[:EDGE] = jnp.zeros((EDGE, block), jnp.float32)
+    for q in range(devices):
+        edges[pl.ds((q + 1) * EDGE, EDGE)] = taken_ref[q, pl.ds(edge, EDGE), :].astype(jnp.float32)
+
+    def ends(index, own):
+        return edges[pl.ds(index + EDGE * own, devices, stride=EDGE), :]
+
+    def first_rows(which):
+        taps = taps_ref[which]
+        base = 2 * (which - 1)
+        now, after = ends(base, 1), ends(base + 1, 1)
+        older, newer = ends(base + 4, 0), ends(base + 5, 0)
+        return (
+            taps[0:1] * now + taps[1:2] * newer + taps[2:3] * older,
+            taps[0:1] * after + taps[1:2] * now + taps[2:3] * newer,
+        )
+
+    key_rows, value_rows = first_rows(1), first_rows(2)
+    first_row, second_row = key_rows[0] * value_rows[0], key_rows[1] * value_rows[1]
+
+    def tokens_of(q):
+        top = taken_ref[q, pl.ds(0, ROWS), :].astype(jnp.float32)
+        index = lax.broadcasted_iota(jnp.int32, top.shape, 0)
+        top = jnp.where(index == 0, first_row[q : q + 1], jnp.where(index == 1, second_row[q : q + 1], top))
+        return jnp.concatenate(
+            [top.astype(jnp.bfloat16), taken_ref[q, pl.ds(ROWS, tokens - ROWS), :]], axis=0
+        )
+
+    def spectrum_rows(start, imag):
+        return pl.ds(tokens + start // GROUP * 2 * GROUP + start % GROUP + imag * GROUP, ROWS)
 
     part = half // RADIX
     matrix = gather_rows(half, RADIX)
     for k in range(0, RADIX, 2):
-        slabs = [taken_ref[2 * k + q, pl.ds(0, tokens), :] for q in range(4)]
+        slabs = [tokens_of(2 * k + q) for q in range(4)]
         both = exact_rows(
             matrix, jnp.concatenate(slabs[:2], axis=0), jnp.concatenate(slabs[2:], axis=0)
         )
@@ -382,6 +427,26 @@
             rows = both[v * part : (v + 1) * part]
             packed[pl.ds(k * part, part), lane[v]] = rows[:, :block]
             packed[pl.ds((k + 1) * part, part), lane[v]] = rows[:, block:]
+
+    row = lax.broadcasted_iota(jnp.int32, (half, half), 0)
+    column = lax.broadcasted_iota(jnp.int32, (half, half), 1)
+    flip = jnp.where(row + column == half, 1.0, 0.0).astype(jnp.bfloat16)
+    for j in range(RADIX):
+        source = 2 * RADIX - 1 - 2 * j
+        right = jnp.concatenate(
+            [
+                jnp.concatenate(
+                    [
+                        taken_ref[source, pl.ds(tokens + (2 * g + imag) * GROUP, GROUP), :]
+                        for g in range(half // GROUP)
+                    ],
+                    axis=0,
+                )
+                for imag in range(2)
+            ],
+            axis=1,
+        )
+        flipped[j] = jnp.dot(flip, right, preferred_element_type=jnp.float32).astype(jnp.bfloat16)
 
     wide = 2 * block
     loads[0].wait()
@@ -393,22 +458,12 @@
             fwd_low[...], right, preferred_element_type=jnp.float32
         )
 
-    row = lax.broadcasted_iota(jnp.int32, (half, half), 0)
-    column = lax.broadcasted_iota(jnp.int32, (half, half), 1)
-    flip = jnp.where(row + column == half, 1.0, 0.0).astype(jnp.bfloat16)
-    for j in range(RADIX):
-        source = 2 * RADIX - 1 - 2 * j
-        right = jnp.concatenate(
-            [taken_ref[source, spectrum_real, :], taken_ref[source, spectrum_imag, :]], axis=1
-        )
-        flipped[j] = jnp.dot(flip, right, preferred_element_type=jnp.float32).astype(jnp.bfloat16)
-
     def products(rows, start, parts):
         parts = butterfly(parts, -1)
         result = []
         for j in range(RADIX):
-            real = taken_ref[2 * j, pl.ds(start + tokens, ROWS), :].astype(jnp.float32)
-            imag = taken_ref[2 * j, pl.ds(start + tokens + half, ROWS), :].astype(jnp.float32)
+            real = taken_ref[2 * j, spectrum_rows(start, 0), :].astype(jnp.float32)
+            imag = taken_ref[2 * j, spectrum_rows(start, 1), :].astype(jnp.float32)
             mirror = flipped[j, rows, :].astype(jnp.float32)
             result.append(scaled(parts[j], (real + mirror[:, :block], imag - mirror[:, block:])))
         return butterfly(result, 1)
@@ -435,8 +490,8 @@
                 scaled(
                     nyquist[j],
                     (
-                        taken_ref[2 * j + 1, pl.ds(tokens, ROWS), :].astype(jnp.float32),
-                        taken_ref[2 * j + 1, pl.ds(tokens + half, ROWS), :].astype(jnp.float32),
+                        taken_ref[2 * j + 1, spectrum_rows(0, 0), :].astype(jnp.float32),
+                        taken_ref[2 * j + 1, spectrum_rows(0, 1), :].astype(jnp.float32),
                     ),
                 )
                 for j in range(RADIX)
@@ -540,7 +595,7 @@
     )()
 
 
-def local_transform(taken, tables, tokens):
+def local_transform(taken, taps, tables, tokens):
     devices, _, block = taken.shape
     length = devices * tokens
     half, depth = length // RADIX, length // RADIX
@@ -551,7 +606,7 @@
     return pl.pallas_call(
         transform_kernel,
         out_shape=pltpu.HBM((devices, tokens, block), jnp.bfloat16),
-        in_specs=[whole] + [remote] * 6,
+        in_specs=[whole] * 2 + [remote] * 6,
         out_specs=remote,
         scratch_shapes=[
             pltpu.VMEM((depth, wide), jnp.bfloat16),
@@ -564,10 +619,11 @@
             pltpu.SemaphoreType.DMA((RADIX // 2,)),
             *(pltpu.VMEM(t.shape, t.dtype) for t in tables),
             pltpu.SemaphoreType.DMA((len(tables),)),
+            pltpu.VMEM(((devices + 1) * EDGE, block), jnp.float32),
         ],
         compiler_params=pltpu.CompilerParams(vmem_limit_bytes=20 * 2**20),
         cost_estimate=pl.CostEstimate(flops=flops, bytes_accessed=taken.size * 2, transcendentals=0),
-    )(taken, *tables)
+    )(taken, taps, *tables)
 
 
 def sum_shares(share, axis):
@@ -585,13 +641,15 @@
 def fused_shards(query, key_in, value, short_taps, skip_gain, filter_spectrum, out_weight):
     devices = lax.axis_size("ctx")
     tokens, channels = query.shape
-    tails = shifted_in(own_tails(query, key_in, value), "ctx")
-    sent = packed_spectrum(filter_spectrum, devices)
-    sent = with_signal(key_in, value, tails, short_taps, sent)
+    block = channels // devices
+    sent = prepared(key_in, value, short_taps, filter_spectrum, devices)
     taken = lax.all_to_all(sent, "ctx", split_axis=0, concat_axis=0, tiled=True)
+    tails = own_tails(query, key_in, value)
+    tails = shifted_in(tails, "ctx")
     gate_signal, direct = gates(query, key_in, value, tails, short_taps, skip_gain)
-    tables = local_tables(tokens * devices, channels // devices)
-    convolved = local_transform(taken, tables, tokens)
+    own_taps = lax.dynamic_slice_in_dim(short_taps, lax.axis_index("ctx") * block, block, axis=2)
+    tables = local_tables(tokens * devices, block)
+    convolved = local_transform(taken, own_taps, tables, tokens)
     convolved = lax.all_to_all(convolved, "ctx", split_axis=0, concat_axis=0, tiled=True)
     return projected(convolved, gate_signal, direct, out_weight)
 

time: 122 us -> 118 us (0.967)
  waiting for transfers between devices: 59.3 us -> 52.9 us
  starting transfers between devices: 25 us -> 27.2 us
    all_to_all x1, waiting for transfers between devices: 11 us -> 6.98 us  [fused_shards(): lax.all_to_all(convolved, 'ctx', split_axis=0, concat_axis=0, tiled=True)]
    ppermute x2 -> x3, waiting for transfers between devices: 7.94 us -> 4.33 us  [projected(): arrived.append(lax.ppermute(far, 'tp', swap))]
    ppermute x2 -> x3, starting transfers between devices: 2.09 us -> 3.65 us  [projected(): arrived.append(lax.ppermute(far, 'tp', swap))]
    unnamed x24 -> x22, local copies, waits for them, and re-layouts: 6.85 us -> 6.84 us
  transfers between devices with their start and end apart: 5 -> 6, of which waited for: 4 -> 5; matrix products, arithmetic and copies ran while one was open for 0% -> 0% of each run, Pallas kernels for 12% -> 11%
where the time goes in v4:
time: 118 us; the launch traced here: 117 us
  waiting for transfers between devices  52.9 us (45%)
  Pallas kernels  29.1 us (25%)
  starting transfers between devices  27.2 us (23%)
  local copies, waits for them, and re-layouts  6.84 us (6%)
    all_to_all x1, waiting for transfers between devices, fused_shards(): taken = lax.all_to_all(sent, 'ctx', split_axis=0, concat_axis=0, tiled=True)  40.9 us
    all_to_all x1, starting transfers between devices, fused_shards(): lax.all_to_all(convolved, 'ctx', split_axis=0, concat_axis=0, tiled=True)  13.5 us
    pallas_call x4, Pallas kernels, share(): pl.pallas_call(kernel, out_shape=(*extra, jax.ShapeDtypeStruct((tokens, w...  10.8 us
    all_to_all x1, starting transfers between devices, fused_shards(): taken = lax.all_to_all(sent, 'ctx', split_axis=0, concat_axis=0, tiled=True)  7.56 us
    all_to_all x1, waiting for transfers between devices, fused_shards(): lax.all_to_all(convolved, 'ctx', split_axis=0, concat_axis=0, tiled=True)  6.98 us
    unnamed x22, local copies, waits for them, and re-layouts  6.84 us
    pallas_call x1, Pallas kernels, local_transform(): pl.pallas_call(transform_kernel, out_shape=pltpu.HBM((devices, tokens, bl...  5.85 us
    pallas_call x1, Pallas kernels, prepared(): pl.pallas_call(prepare_kernel, out_shape=pltpu.HBM((devices, rows, block)...  5.41 us
  transfers between devices with their start and end apart: 6, of which 5 were waited for; matrix products, arithmetic and copies ran while one was open for 0% of the time, Pallas kernels for 11%

profile of v4, /device:TPU:0, one launch (start us, length us, event | category | flops | bytes accessed | tf_op | source)
XLA Modules:
  0.0 117.0 jit_solution(16505445005252982164)
XLA Ops:
  0.0 5.4 %shard_map.73 = bf16[16,648,128]{2,1,0:T(8,128)(2,1)} custom-call(f32[8192,128]{1,0:T(8,128)} %bitcast.7, bf16[128,2048]{1,0:T(8,128)(2,1)} %key_ref.5, bf16[128,2048]{1,0:T(8,128)(2,1)} %value_ref.5, f32[3,3,2048]{2,1,0:T(4,128)} %taps_ref.3), custom_call_target="tpu_custom_call" | custom-call | bytes 6291456 | tf_op jit(solution)/shard_map/pallas_call | solution.py:206
  5.4 7.6 %all-to-all-start = ((bf16[16,648,128]{2,1,0:T(8,128)(2,1)}), bf16[16,648,128]{2,1,0:T(8,128)(2,1)S(1)}, u32[]{:S(2)}, u32[]{:S(2)}) async-start(bf16[16,648,128]{2,1,0:T(8,128)(2,1)} %shard_map.73), calls=%async_computation | async-start | bytes 5308416 | tf_op jit(solution)/shard_map/all_to_all | solution.py:646
  13.0 5.0 %shard_map.74 = (bf16[512,256]{1,0:T(8,128)(2,1)S(1)}, bf16[512,256]{1,0:T(8,128)(2,1)S(1)}, bf16[256,512]{1,0:T(8,128)(2,1)S(1)}, bf16[256,512]{1,0:T(8,128)(2,...) custom-call(), custom_call_target="tpu_custom_call" | custom-call | flops 52428800 | bytes 2097152 | tf_op jit(solution)/shard_map/pallas_call | solution.py:587
  18.0 1.0 copy-done.3
  19.0 1.0 copy-done.4
  20.7 0.7 copy-done.7
  22.8 40.9 %all-to-all-done.taken_ref = bf16[16,648,128]{2,1,0:T(8,128)(2,1)S(1)} async-done(((bf16[16,648,128]{2,1,0:T(8,128)(2,1)}), bf16[16,648,128]{2,1,0:T(8,128)(2,1)S(1)}, u32[]{:S(2)}, u32[]{:S(2)}) %all-to-all-start) | async-done | bytes 2654240 | tf_op jit(solution)/shard_map/all_to_all | solution.py:646
  63.7 5.9 %shard_map.75 = bf16[16,128,128]{2,1,0:T(8,128)(2,1)} custom-call(bf16[16,648,128]{2,1,0:T(8,128)(2,1)S(1)} %all-to-all-done.taken_ref, f32[3,3,128]{2,1,0:T(4,128)S(1)} %constant_dynamic-slice_fusion.taps_ref, bf16[512,256]{1,0:T(8,128)(2,1)} %copy-done.6, bf16[512,256]{1,0:T(8,128)(2,1)} %copy-done.7, bf16[256,512]{1,0:T(8,128)(2,1)} %copy-done.8, ...), custom_call_target="tpu_custom_call" | custom-call | flops 1342177280 | bytes 2654208 | tf_op jit(solution)/shard_map/pallas_call | solution.py:606
  69.5 13.5 %all-to-all-start.1 = ((bf16[16,128,128]{2,1,0:T(8,128)(2,1)}), bf16[16,128,128]{2,1,0:T(8,128)(2,1)S(1)}, u32[]{:S(2)}, u32[]{:S(2)}) async-start(bf16[16,128,128]{2,1,0:T(8,128)(2,1)} %shard_map.75), calls=%async_computation.1 | async-start | bytes 1048576 | tf_op jit(solution)/shard_map/all_to_all | solution.py:653
  83.0 0.9 shard_map.76
  83.9 2.5 %collective-permute-start = (bf16[6,2048]{1,0:T(8,128)(2,1)S(1)}, bf16[6,2048]{1,0:T(8,128)(2,1)S(1)}, u32[]{:S(2)}, u32[]{:S(2)}) collective-permute-start(bf16[6,2048]{1,0:T(8,128)(2,1)S(1)} %shard_map.76), channel_id=1, source_target_pairs={{0,2},{2,4},{4,6},{6,8},{8,10},{10,12},{12,14},{14,16},{16,18},{18... | collective-permute-start | bytes 73736 | tf_op jit(solution)/shard_map/ppermute | solution.py:23
  87.1 1.0 copy-done.1
  88.1 1.0 copy-done.2
  89.2 1.1 shard_map.77
  90.3 7.0 %all-to-all-done.1.conv_ref = bf16[16,128,128]{2,1,0:T(8,128)(2,1)S(1)} async-done(((bf16[16,128,128]{2,1,0:T(8,128)(2,1)}), bf16[16,128,128]{2,1,0:T(8,128)(2,1)S(1)}, u32[]{:S(2)}, u32[]{:S(2)}) %all-to-all-start.1) | async-done | bytes 524320 | tf_op jit(solution)/shard_map/all_to_all | solution.py:653
  97.3 2.1 %shard_map.78 = (bf16[128,2048]{1,0:T(8,128)(2,1)S(1)}, bf16[128,512]{1,0:T(8,128)(2,1)S(1)}) custom-call(bf16[16,128,128]{2,1,0:T(8,128)(2,1)S(1)} %all-to-all-done.1.conv_ref, f32[128,2048]{1,0:T(8,128)S(1)} %get-tuple-element.21.gate_ref, f32[128,2048]{1,0:T(8,128)S(1)} %get-tuple-element.22.direct_ref, bf16[2048,4096]{1,0:T(8,128)(2,1)} %weight_ref.7), custom_call_target="tpu_custom_call" | custom-call | flops 268435456 | bytes 2097152 | tf_op jit(solution)/shard_map/pallas_call | solution.py:302
  99.4 2.7 %shard_map.81 = bf16[128,1024]{1,0:T(8,128)(2,1)S(1)} custom-call(bf16[128,2048]{1,0:T(8,128)(2,1)S(1)} %get-tuple-element.23.gated_ref, bf16[2048,4096]{1,0:T(8,128)(2,1)} %weight_ref.7), custom_call_target="tpu_custom_call" | custom-call | flops 536870912 | bytes 4194304 | tf_op jit(solution)/shard_map/pallas_call | solution.py:302
  102.1 1.6 %collective-permute-start.3 = (bf16[128,1024]{1,0:T(8,128)(2,1)S(1)}, bf16[128,1024]{1,0:T(8,128)(2,1)S(1)}, u32[]{:S(2)}, u32[]{:S(2)}) collective-permute-start(bf16[128,1024]{1,0:T(8,128)(2,1)S(1)} %shard_map.81), channel_id=1, source_target_pairs={{0,1},{1,0},{2,3},{3,2},{4,5},{5,4},{6,7},{7,6},{8,9},{9,8},{10,11... | collective-permute-start | bytes 786440 | tf_op jit(solution)/shard_map/ppermute | solution.py:333
  103.6 2.0 %shard_map.80 = bf16[128,512]{1,0:T(8,128)(2,1)S(1)} custom-call(bf16[128,2048]{1,0:T(8,128)(2,1)S(1)} %get-tuple-element.23.gated_ref, bf16[2048,4096]{1,0:T(8,128)(2,1)} %weight_ref.7), custom_call_target="tpu_custom_call" | custom-call | flops 268435456 | bytes 2097152 | tf_op jit(solution)/shard_map/pallas_call | solution.py:302
  106.3 1.5 %collective-permute-start.1 = (bf16[128,512]{1,0:T(8,128)(2,1)S(1)}, bf16[128,512]{1,0:T(8,128)(2,1)S(1)}, u32[]{:S(2)}, u32[]{:S(2)}) collective-permute-start(bf16[128,512]{1,0:T(8,128)(2,1)S(1)} %get-tuple-element.24), channel_id=1, source_target_pairs={{0,1},{1,0},{2,3},{3,2},{4,5},{5,4},{6,7},{7,6},{8,9},{9,8},{10,11... | collective-permute-start | bytes 393224 | tf_op jit(solution)/shard_map/ppermute | solution.py:333
  107.8 4.0 %shard_map.79 = f32[128,2048]{1,0:T(8,128)S(1)} custom-call(bf16[128,2048]{1,0:T(8,128)(2,1)S(1)} %get-tuple-element.23.gated_ref, bf16[2048,4096]{1,0:T(8,128)(2,1)} %weight_ref.7), custom_call_target="tpu_custom_call" | custom-call | flops 1073741824 | bytes 8388608 | tf_op jit(solution)/shard_map/pallas_call | solution.py:302
  111.8 2.3 %collective-permute-done.2 = bf16[128,512]{1,0:T(8,128)(2,1)S(1)} collective-permute-done((bf16[128,512]{1,0:T(8,128)(2,1)S(1)}, bf16[128,512]{1,0:T(8,128)(2,1)S(1)}, u32[]{:S(2)}, u32[]{:S(2)}) %collective-permute-start.2) | collective-permute-done | bytes 131104 | tf_op jit(solution)/shard_map/ppermute | solution.py:333
  114.1 2.0 %collective-permute-done.1 = bf16[128,512]{1,0:T(8,128)(2,1)S(1)} collective-permute-done((bf16[128,512]{1,0:T(8,128)(2,1)S(1)}, bf16[128,512]{1,0:T(8,128)(2,1)S(1)}, u32[]{:S(2)}, u32[]{:S(2)}) %collective-permute-start.1) | collective-permute-done | bytes 131104 | tf_op jit(solution)/shard_map/ppermute | solution.py:333
  116.1 0.9 add_convert_fusion
  (21 shorter events, 3.4 us)
Async XLA Ops:
  5.4 17.3 %copy-start.5 = (f32[3,3,2048]{2,1,0:T(4,128)S(1)}, f32[3,3,2048]{2,1,0:T(4,128)}, u32[]{:S(2)}) copy-start(f32[3,3,2048]{2,1,0:T(4,128)} %taps_ref.3) | copy-start | bytes 221188
  5.4 58.2 %all-to-all-start = ((bf16[16,648,128]{2,1,0:T(8,128)(2,1)}), bf16[16,648,128]{2,1,0:T(8,128)(2,1)S(1)}, u32[]{:S(2)}, u32[]{:S(2)}) async-start(bf16[16,648,128]{2,1,0:T(8,128)(2,1)} %shard_map.73), calls=%async_computation | async-start | bytes 5308416 | tf_op jit(solution)/shard_map/all_to_all | solution.py:646
  18.0 1.0 copy-start.3
  19.0 1.0 copy-start.4
  20.0 0.7 copy-start.6
  20.7 0.7 copy-start.7
  21.4 0.7 copy-start.8
  22.1 0.7 copy-start.9
  63.7 23.4 %copy-start = (bf16[128,2048]{1,0:T(8,128)(2,1)S(1)}, bf16[128,2048]{1,0:T(8,128)(2,1)}, u32[]{:S(2)}) copy-start(bf16[128,2048]{1,0:T(8,128)(2,1)} %key_ref.5) | copy-start | bytes 1572868
  63.7 23.4 %copy-start.10 = (f32[2048]{0:T(1024)S(1)}, f32[2048]{0:T(1024)}, u32[]{:S(2)}) copy-start(f32[2048]{0:T(1024)} %param.11) | copy-start | bytes 24580
  69.5 27.7 %all-to-all-start.1 = ((bf16[16,128,128]{2,1,0:T(8,128)(2,1)}), bf16[16,128,128]{2,1,0:T(8,128)(2,1)S(1)}, u32[]{:S(2)}, u32[]{:S(2)}) async-start(bf16[16,128,128]{2,1,0:T(8,128)(2,1)} %shard_map.75), calls=%async_computation.1 | async-start | bytes 1048576 | tf_op jit(solution)/shard_map/all_to_all | solution.py:653
  83.9 3.2 %collective-permute-start = (bf16[6,2048]{1,0:T(8,128)(2,1)S(1)}, bf16[6,2048]{1,0:T(8,128)(2,1)S(1)}, u32[]{:S(2)}, u32[]{:S(2)}) collective-permute-start(bf16[6,2048]{1,0:T(8,128)(2,1)S(1)} %shard_map.76), channel_id=1, source_target_pairs={{0,2},{2,4},{4,6},{6,8},{8,10},{10,12},{12,14},{14,16},{16,18},{18... | collective-permute-start | bytes 73736 | tf_op jit(solution)/shard_map/ppermute | solution.py:23
  87.1 1.0 copy-start.1
  88.1 1.0 copy-start.2
  102.1 14.0 %collective-permute-start.3 = (bf16[128,1024]{1,0:T(8,128)(2,1)S(1)}, bf16[128,1024]{1,0:T(8,128)(2,1)S(1)}, u32[]{:S(2)}, u32[]{:S(2)}) collective-permute-start(bf16[128,1024]{1,0:T(8,128)(2,1)S(1)} %shard_map.81), channel_id=1, source_target_pairs={{0,1},{1,0},{2,3},{3,2},{4,5},{5,4},{6,7},{7,6},{8,9},{9,8},{10,11... | collective-permute-start | bytes 786440 | tf_op jit(solution)/shard_map/ppermute | solution.py:333
  105.7 8.4 %collective-permute-start.2 = (bf16[128,512]{1,0:T(8,128)(2,1)S(1)}, bf16[128,512]{1,0:T(8,128)(2,1)S(1)}, u32[]{:S(2)}, u32[]{:S(2)}) collective-permute-start(bf16[128,512]{1,0:T(8,128)(2,1)S(1)} %shard_map.80), channel_id=1, source_target_pairs={{0,1},{1,0},{2,3},{3,2},{4,5},{5,4},{6,7},{7,6},{8,9},{9,8},{10,11... | collective-permute-start | bytes 393224 | tf_op jit(solution)/shard_map/ppermute | solution.py:333
  106.3 9.8 %collective-permute-start.1 = (bf16[128,512]{1,0:T(8,128)(2,1)S(1)}, bf16[128,512]{1,0:T(8,128)(2,1)S(1)}, u32[]{:S(2)}, u32[]{:S(2)}) collective-permute-start(bf16[128,512]{1,0:T(8,128)(2,1)S(1)} %get-tuple-element.24), channel_id=1, source_target_pairs={{0,1},{1,0},{2,3},{3,2},{4,5},{5,4},{6,7},{7,6},{8,9},{9,8},{10,11... | collective-permute-start | bytes 393224 | tf_op jit(solution)/shard_map/ppermute | solution.py:333
